TPU v7x, 256 devices: a whole 4x4x8 slice. The times are simulated.
256 devices in a mesh: ang: 8 (over x_hi, y), strip: 32 (over x_lo, z, core).
Axes of the slice: x: 4 (x_hi: 2, x_lo: 2; x = x_hi * 2 + x_lo), y: 4, z: 8, core: 2. Of those that a mesh axis runs over, the one named last changes fastest.
Arguments:
- slab: bfloat16 [8, 2, 4096, 512], P('ang', None, 'strip'), may hold values from -6 to 6
- shear_taps: float32 [4, 8, 8], replicated, may hold values from -1 to 1
- band_offsets: int32 [8, 8], replicated, may hold values from -64 to 64
- probe: bfloat16 [2, 256, 256], replicated, may hold values from -6 to 6
- scan_rows: int32 [8, 128], P('ang', 'strip'), may hold values from 0 to 127
- scan_columns: int32 [8, 128], P('ang', 'strip'), may hold values from 0 to 256
- frame_counts: int32 [8, 32], P('ang', 'strip'), may hold values from 1 to 4, 64 in all within a row
- amplitudes: bfloat16 [8, 128, 256, 256], P('ang', 'strip'), may hold values from 0.19921875 to 4
Outputs:
- slab_grad: float32 [8, 2, 4096, 512], P('ang', None, 'strip')
Inputs may be any that keep to these rules, and one draw needn't show every extreme that they name: `frame_counts`: for every angle the counts over the 32 strips sum to 64, and some strip has exactly 4 frames.
All inputs are finite; a program needn't handle non-finite values. No bound on the sum of `frame_counts` on one device may be relied on, other than what follows from the above.
Results may differ from a plain program's by a relative error of at most 0.013.
Values may be sent and summed in bfloat16 or wider, within the bound.
No kernel may reach another device: no remote copies, remote signals or barrier semaphores. Data moves between devices by JAX's collectives and lax.ppermute only.
A program may use at most 64 MiB of HBM per device.

v0:
```python
import functools
import math

import jax
import jax.numpy as jnp
import numpy as np
from jax import lax
from jax.experimental import pallas as pl
from jax.experimental.pallas import tpu as pltpu
from jax.sharding import PartitionSpec as P

MAXSHIFT = 64
LANES = 128
MROWS = 256
CHUNK = 256
VMEM = pltpu.VMEM
SMEM = pltpu.SMEM


def dft_blocks(length):
    index = np.arange(length, dtype=np.int64)
    product = index[:, None] * index[None, :] % length
    phase = product.astype(np.float32) * np.float32(2.0 * math.pi / length)
    scale = np.float32(1.0 / math.sqrt(length))
    cosine = (np.cos(phase) * scale).astype(jnp.bfloat16)
    sine = (np.sin(phase) * scale).astype(jnp.bfloat16)
    forward = np.block([[cosine, sine], [-sine, cosine]])
    inverse = np.block([[cosine, -sine], [sine, cosine]])
    return forward, inverse


def in_hbm(x):
    return pltpu.with_memory_space_constraint(x, pltpu.HBM)


def lane_index(shape):
    return lax.broadcasted_iota(jnp.int32, shape, len(shape) - 1)


def shear_body(sign, taps_hbm, offsets_hbm, x_ref, o_ref, taps_ref, offsets_ref, ready, copies):
    count, rows, width = x_ref.shape
    tiles = width // LANES + 1
    ntaps = taps_ref.shape[0]
    left = MAXSHIFT if sign > 0 else MAXSHIFT + ntaps - 1
    get_taps = pltpu.make_async_copy(taps_hbm, taps_ref, ready.at[0])
    get_offsets = pltpu.make_async_copy(offsets_hbm, offsets_ref, ready.at[1])
    get_taps.start()
    get_offsets.start()

    def lay_out(s, _):
        value = x_ref[s].astype(jnp.float32)
        value = jnp.concatenate([value, jnp.zeros((rows, LANES), jnp.float32)], axis=1)
        for k in range(ntaps):
            moved = pltpu.roll(value, left - k, axis=1)
            for j in range(tiles):
                copies[s, k, j] = moved[:, j * LANES : (j + 1) * LANES]
        return 0

    lax.fori_loop(0, count, lay_out, 0)
    get_taps.wait()
    get_offsets.wait()
    lane = lane_index((rows, LANES))

    def one(d, _):
        total = [jnp.zeros((rows, LANES), jnp.float32) for _ in range(tiles - 1)]
        for s in range(count):
            angle, depth = (d, s) if sign > 0 else (s, d)
            amount = MAXSHIFT + sign * offsets_ref[angle, depth]
            back = lax.rem(LANES - amount, LANES)
            keep = lane < LANES - amount
            weights = [taps_ref[k if sign > 0 else ntaps - 1 - k, angle, depth] for k in range(ntaps)]
            turned = []
            for j in range(tiles):
                terms = [weights[k] * copies[s, k, j] for k in range(ntaps)]
                both = (terms[0] + terms[1]) + (terms[2] + terms[3])
                turned.append(pltpu.roll(both, back, axis=1))
            for j in range(tiles - 1):
                total[j] = total[j] + jnp.where(keep, turned[j], turned[j + 1])
        for j in range(tiles - 1):
            o_ref[d, :, pl.ds(j * LANES, LANES)] = total[j].astype(o_ref.dtype)
        return 0

    lax.fori_loop(0, count, one, 0)


def shear(x, taps, offsets, sign):
    count, rows, width = x.shape
    tiles = width // LANES + 1
    return pl.pallas_call(
        functools.partial(shear_body, sign),
        out_shape=jax.ShapeDtypeStruct(x.shape, jnp.bfloat16),
        in_specs=[
            pl.BlockSpec(memory_space=pltpu.HBM),
            pl.BlockSpec(memory_space=pltpu.HBM),
            pl.BlockSpec(memory_space=VMEM),
        ],
        out_specs=pl.BlockSpec(memory_space=VMEM),
        scratch_shapes=[
            SMEM(taps.shape, taps.dtype),
            SMEM(offsets.shape, offsets.dtype),
            pltpu.SemaphoreType.DMA((2,)),
            VMEM((count, taps.shape[0], tiles, rows, LANES), jnp.float32),
        ],
        compiler_params=pltpu.CompilerParams(vmem_limit_bytes=16 << 20),
        name="shear_forward" if sign > 0 else "shear_back",
    )(in_hbm(taps), in_hbm(offsets), x)


def frames_body(
    odd_ref, counts_ref, rows_hbm, columns_hbm, own_ref, near_ref, far_ref, probe_hbm, amp_ref, fwd_ref, inv_ref,
    mid_ref, to_near_ref, to_far_ref,
    ready, rows_ref, columns_ref, probe_ref, ext, placed,
    column_a, column_b, side_a, side_b, wave_a,
):
    length = probe_ref.shape[1]
    strip = own_ref.shape[1]
    width = own_ref.shape[2]
    gets = [
        pltpu.make_async_copy(src, dst, ready.at[i])
        for i, (src, dst) in enumerate(
            [(rows_hbm, rows_ref), (columns_hbm, columns_ref), (probe_hbm, probe_ref)]
        )
    ]
    for get in gets:
        get.start()
    odd = odd_ref[0]
    near_row = pl.multiple_of((1 - odd) * 2 * strip, strip)
    far_row = pl.multiple_of(odd * 2 * strip, strip)
    tiles = width // LANES
    for p in range(2):
        for j in range(tiles):
            tile = pl.ds(j * LANES, LANES)
            ext[p, j, pl.ds(strip, strip), :] = own_ref[p, :, tile].astype(jnp.float32)
            ext[p, j, pl.ds(near_row, strip), :] = near_ref[p, :, tile].astype(jnp.float32)
            ext[p, j, pl.ds(far_row, strip), :] = far_ref[p, :, tile].astype(jnp.float32)
    placed[...] = jnp.zeros_like(placed)
    wave_a[...] = jnp.zeros_like(wave_a)
    for get in gets:
        get.wait()
    part = 16
    lane = lane_index((part, LANES))
    count = counts_ref[0, 0]
    slots = amp_ref.shape[0]
    spots = range(0, length, part)

    def place_of(f):
        col = columns_ref[0, f]
        return rows_ref[0, f], col // LANES, lax.rem(col, LANES)

    def cut(f, column):
        row, first, rest = place_of(f)
        back = lax.rem(LANES - rest, LANES)
        low = lane < LANES - rest
        for at in spots:
            window = []
            for p in range(2):
                turned = [pltpu.roll(ext[p, first + j, pl.ds(row + at, part), :], back, axis=1) for j in range(3)]
                window.append([jnp.where(low, turned[j], turned[j + 1]) for j in range(2)])
            for j in range(2):
                tile = pl.ds(j * LANES, LANES)
                pr = probe_ref[0, pl.ds(at, part), tile].astype(jnp.float32)
                pi = probe_ref[1, pl.ds(at, part), tile].astype(jnp.float32)
                xr, xi = window[0][j], window[1][j]
                column[pl.ds(at, part), tile] = (pr * xr - pi * xi).astype(jnp.bfloat16)
                column[pl.ds(length + at, part), tile] = (pr * xi + pi * xr).astype(jnp.bfloat16)

    def left(matrix, column, side):
        for m in range(0, 2 * length, MROWS):
            value = jnp.dot(matrix[pl.ds(m, MROWS), :], column[...], preferred_element_type=jnp.float32)
            p, r = divmod(m, length)
            if MROWS > length:
                side[:, pl.ds(0, length)] = value[:length].astype(jnp.bfloat16)
                side[:, pl.ds(length, length)] = value[length:].astype(jnp.bfloat16)
            else:
                side[pl.ds(r, MROWS), pl.ds(p * length, length)] = value.astype(jnp.bfloat16)

    def compare(f, side, column):
        for at in spots:
            if at % CHUNK == 0:
                far = jnp.dot(side[pl.ds(at, CHUNK), :], inv_ref[...], preferred_element_type=jnp.float32)
            rs = slice(at % CHUNK, at % CHUNK + part)
            fr = far[rs, :length]
            fi = far[rs, length:]
            factor = 1.0 - amp_ref[f, pl.ds(at, part), :].astype(jnp.float32) * lax.rsqrt(fr * fr + fi * fi + 1.0)
            column[pl.ds(at, part), :] = (fr * factor).astype(jnp.bfloat16)
            column[pl.ds(length + at, part), :] = (fi * factor).astype(jnp.bfloat16)

    def turn_back(f, side, wave):
        rest = place_of(f)[2]
        for at in spots:
            if at % CHUNK == 0:
                back = jnp.dot(side[pl.ds(at, CHUNK), :], fwd_ref[...], preferred_element_type=jnp.float32)
            rs = slice(at % CHUNK, at % CHUNK + part)
            for j in range(2):
                tile = pl.ds(j * LANES, LANES)
                pr = probe_ref[0, pl.ds(at, part), tile].astype(jnp.float32)
                pi = probe_ref[1, pl.ds(at, part), tile].astype(jnp.float32)
                br = back[rs, j * LANES : (j + 1) * LANES]
                bi = back[rs, length + j * LANES : length + (j + 1) * LANES]
                wave[0, j, pl.ds(at, part), :] = pltpu.roll(pr * br + pi * bi, rest, axis=1)
                wave[1, j, pl.ds(at, part), :] = pltpu.roll(pr * bi - pi * br, rest, axis=1)

    def add(f, wave):
        row, first, rest = place_of(f)
        high = lane >= rest
        for at in spots:
            for p in range(2):
                one = wave[p, 0, pl.ds(at, part), :]
                two = wave[p, 1, pl.ds(at, part), :]
                pieces = [jnp.where(high, one, 0.0), jnp.where(high, two, one), jnp.where(high, 0.0, two)]
                for j in range(3):
                    spot = (p, first + j, pl.ds(row + at, part), slice(None))
                    placed[spot] = placed[spot] + pieces[j]

    def one_frame(f, _):
        left(fwd_ref, column_a, side_a)
        cut(jnp.minimum(f + 1, slots - 1), column_a)
        add(jnp.maximum(f - 1, 0), wave_a)
        compare(f, side_a, column_b)
        left(inv_ref, column_b, side_b)
        turn_back(f, side_b, wave_a)
        return 0

    cut(0, column_a)
    lax.fori_loop(0, count, one_frame, 0)
    add(count - 1, wave_a)
    for p in range(2):
        for j in range(tiles):
            tile = pl.ds(j * LANES, LANES)
            mid_ref[p, :, tile] = placed[p, j, pl.ds(strip, strip), :]
            to_near_ref[p, :, tile] = placed[p, j, pl.ds(near_row, strip), :].astype(to_near_ref.dtype)
            to_far_ref[p, :, tile] = placed[p, j, pl.ds(far_row, strip), :].astype(to_far_ref.dtype)


def frames(odd, rows, columns, counts, own, near, far, probe, amplitudes):
    length = probe.shape[1]
    parts, strip, width = own.shape
    fwd, inv = (jnp.asarray(m) for m in dft_blocks(length))
    hbm = pl.BlockSpec(memory_space=pltpu.HBM)
    vmem = pl.BlockSpec(memory_space=VMEM)
    return pl.pallas_call(
        frames_body,
        out_shape=(
            jax.ShapeDtypeStruct(own.shape, jnp.float32),
            jax.ShapeDtypeStruct(own.shape, jnp.bfloat16),
            jax.ShapeDtypeStruct(own.shape, jnp.bfloat16),
        ),
        in_specs=[pl.BlockSpec(memory_space=SMEM)] * 2 + [hbm] * 2 + [vmem] * 3 + [hbm] + [vmem] * 3,
        out_specs=(vmem,) * 3,
        scratch_shapes=[
            pltpu.SemaphoreType.DMA((3,)),
            SMEM(rows.shape, rows.dtype),
            SMEM(columns.shape, columns.dtype),
            VMEM(probe.shape, probe.dtype),
            VMEM((parts, width // LANES + 1, 3 * strip, LANES), jnp.float32),
            VMEM((parts, width // LANES + 1, 3 * strip, LANES), jnp.float32),
            VMEM((2 * length, length), jnp.bfloat16),
            VMEM((2 * length, length), jnp.bfloat16),
            VMEM((length, 2 * length), jnp.bfloat16),
            VMEM((length, 2 * length), jnp.bfloat16),
            VMEM((2, length // LANES, length, LANES), jnp.float32),
        ],
        compiler_params=pltpu.CompilerParams(vmem_limit_bytes=32 << 20),
        name="frames",
    )(odd, counts, in_hbm(rows), in_hbm(columns), own, near, far, in_hbm(probe), amplitudes, fwd, inv)


def per_device(slab, taps, offsets, probe, scan_rows, scan_columns, counts, amplitudes):
    parts, rows, width = slab.shape[1:]
    angles = lax.axis_size("ang")
    strips = lax.axis_size("strip")
    block = parts * rows // angles
    me = lax.axis_index("strip")

    def swap(x, partner):
        route = [(s, partner(s)) for s in range(strips) if 0 <= partner(s) < strips]
        return lax.ppermute(x, "strip", route)

    def near(x):
        return swap(x, lambda s: s ^ 1)

    def far(x):
        return swap(x, lambda s: s + 1 if s % 2 else s - 1)

    def exchange(x):
        return lax.all_to_all(x, "ang", 0, 0, tiled=True)

    mixed = exchange(slab.reshape(angles, block, width))
    projection = exchange(shear(mixed, taps, offsets, 1)).reshape(parts, rows, width)
    odd = (me & 1).astype(jnp.int32).reshape(1)
    mid, to_near, to_far = frames(
        odd, scan_rows, scan_columns, counts, projection, near(projection), far(projection), probe, amplitudes[0]
    )
    image = mid + near(to_near).astype(jnp.float32) + far(to_far).astype(jnp.float32)
    mixed = exchange(image.astype(jnp.bfloat16).reshape(angles, block, width))
    result = exchange(shear(mixed, taps, offsets, -1))
    return result.reshape(1, parts, rows, width).astype(jnp.float32)


def solution(mesh):
    return jax.shard_map(
        per_device,
        mesh=mesh,
        in_specs=(
            P("ang", None, "strip", None),
            P(),
            P(),
            P(),
            P("ang", "strip"),
            P("ang", "strip"),
            P("ang", "strip"),
            P("ang", "strip", None, None),
        ),
        out_specs=P("ang", None, "strip", None),
        check_vma=False,
    )
```

profile of v0, /device:TPU:2, one launch (start us, length us, event | category | flops | bytes accessed | tf_op | source)
XLA Modules:
  0.0 81.6 jit_solution(18240276001537051648)
XLA Ops:
  0.0 0.0 copy-start.2
  0.0 14.9 %all_to_all.20.x_ref = bf16[8,32,512]{2,1,0:T(8,128)(2,1)S(1)} all-to-all(bf16[8,32,512]{2,1,0:T(8,128)(2,1)} %bitcast.13), channel_id=1, replica_groups=mesh['ang'=8,'strip'=32] {'ang'}, dimensions={0} | all-to-all | bytes 524288 | tf_op jit(solution)/shard_map/all_to_all | solution.py:286
  14.9 0.0 copy-start
  14.9 0.0 copy-start.1
  14.9 3.2 %shear_forward.1 = bf16[8,32,512]{2,1,0:T(8,128)(2,1)S(1)} custom-call(f32[4,8,8]{2,1,0:T(8,128)} %taps_hbm.3, s32[8,8]{1,0:T(8,128)} %offsets_hbm.3, bf16[8,32,512]{2,1,0:T(8,128)(2,1)S(1)} %all_to_all.20.x_ref), custom_call_target="tpu_custom_call" | custom-call | tf_op jit(solution)/shard_map/shear_forward/pallas_call | solution.py:89
  18.1 11.3 %all_to_all.21 = bf16[8,32,512]{2,1,0:T(8,128)(2,1)S(1)} all-to-all(bf16[8,32,512]{2,1,0:T(8,128)(2,1)S(1)} %shear_forward.1), channel_id=1, replica_groups=mesh['ang'=8,'strip'=32] {'ang'}, dimensions={0} | all-to-all | bytes 524288 | tf_op jit(solution)/shard_map/all_to_all | solution.py:286
  29.4 5.7 %collective-permute-start.1 = (bf16[2,128,512]{2,1,0:T(8,128)(2,1)S(1)}, bf16[2,128,512]{2,1,0:T(8,128)(2,1)S(1)}, u32[]{:S(2)}, u32[]{:S(2)}) collective-permute-start(bf16[2,128,512]{2,1,0:T(8,128)(2,1)S(1)} %bitcast.7), channel_id=1, source_target_pairs={{1,2},{2,1},{3,4},{4,3},{5,6},{6,5},{7,8},{8,7},{9,10},{10,9},{11,... | collective-permute-start | bytes 786440 | tf_op jit(solution)/shard_map/ppermute | solution.py:277
  35.1 0.1 collective-permute-start
  35.8 3.4 %collective-permute-done.1.far_ref = bf16[2,128,512]{2,1,0:T(8,128)(2,1)S(1)} collective-permute-done((bf16[2,128,512]{2,1,0:T(8,128)(2,1)S(1)}, bf16[2,128,512]{2,1,0:T(8,128)(2,1)S(1)}, u32[]{:S(2)}, u32[]{:S(2)}) %collective-permute-start.1) | collective-permute-done | bytes 262176 | tf_op jit(solution)/shard_map/ppermute | solution.py:277
  39.2 0.0 collective-permute-done.near_ref
  39.2 0.0 copy-done.2
  39.2 0.0 copy-done
  39.2 0.0 copy-done.1
  39.2 4.0 %frames.1 = (f32[2,128,512]{2,1,0:T(8,128)S(1)}, bf16[2,128,512]{2,1,0:T(8,128)(2,1)S(1)}, bf16[2,128,512]{2,1,0:T(8,128)(2,1)S(1)}) custom-call(s32[1]{0:T(128)} %bitcast.odd_ref, s32[1,1]{1,0:T(1,128)S(6)} %copy.11.counts_ref, s32[1,4]{1,0:T(1,128)} %rows_hbm.1, s32[1,4]{1,0:T(1,128)} %columns_hbm.1, bf16[2,128,512]{2,1,0:T(8,128)(2,1)S(1)} %bitcast.9, ...), custom_call_target="tpu_custom_call" | custom-call | tf_op jit(solution)/shard_map/frames/pallas_call | solution.py:241
  43.2 1.1 %collective-permute-start.2 = (bf16[2,128,512]{2,1,0:T(8,128)(2,1)S(1)}, bf16[2,128,512]{2,1,0:T(8,128)(2,1)S(1)}, u32[]{:S(2)}, u32[]{:S(2)}) collective-permute-start(bf16[2,128,512]{2,1,0:T(8,128)(2,1)S(1)} %get-tuple-element.9), channel_id=1, source_target_pairs={{0,1},{1,0},{2,3},{3,2},{4,5},{5,4},{6,7},{7,6},{8,9},{9,8},{10,11... | collective-permute-start | bytes 786440 | tf_op jit(solution)/shard_map/ppermute | solution.py:277
  44.3 4.4 %collective-permute-start.3 = (bf16[2,128,512]{2,1,0:T(8,128)(2,1)S(1)}, bf16[2,128,512]{2,1,0:T(8,128)(2,1)S(1)}, u32[]{:S(2)}, u32[]{:S(2)}) collective-permute-start(bf16[2,128,512]{2,1,0:T(8,128)(2,1)S(1)} %get-tuple-element.10), channel_id=1, source_target_pairs={{1,2},{2,1},{3,4},{4,3},{5,6},{6,5},{7,8},{8,7},{9,10},{10,9},{11,... | collective-permute-start | bytes 786440 | tf_op jit(solution)/shard_map/ppermute | solution.py:277
  48.7 0.0 collective-permute-done.2
  48.7 5.4 %collective-permute-done.3 = bf16[2,128,512]{2,1,0:T(8,128)(2,1)S(1)} collective-permute-done((bf16[2,128,512]{2,1,0:T(8,128)(2,1)S(1)}, bf16[2,128,512]{2,1,0:T(8,128)(2,1)S(1)}, u32[]{:S(2)}, u32[]{:S(2)}) %collective-permute-start.3) | collective-permute-done | bytes 262176 | tf_op jit(solution)/shard_map/ppermute | solution.py:277
  54.1 0.1 add_convert_fusion
  54.2 12.2 %all_to_all.22.x_ref = bf16[8,32,512]{2,1,0:T(8,128)(2,1)S(1)} all-to-all(bf16[8,32,512]{2,1,0:T(8,128)(2,1)S(1)} %bitcast.11), channel_id=1, replica_groups=mesh['ang'=8,'strip'=32] {'ang'}, dimensions={0} | all-to-all | bytes 524288 | tf_op jit(solution)/shard_map/all_to_all | solution.py:286
  66.4 3.0 %shear_back.1 = bf16[8,32,512]{2,1,0:T(8,128)(2,1)S(1)} custom-call(f32[4,8,8]{2,1,0:T(8,128)} %taps_hbm.3, s32[8,8]{1,0:T(8,128)} %offsets_hbm.3, bf16[8,32,512]{2,1,0:T(8,128)(2,1)S(1)} %all_to_all.22.x_ref), custom_call_target="tpu_custom_call" | custom-call | tf_op jit(solution)/shard_map/shear_back/pallas_call | solution.py:89
  69.4 11.3 %all_to_all.23 = bf16[8,32,512]{2,1,0:T(8,128)(2,1)S(1)} all-to-all(bf16[8,32,512]{2,1,0:T(8,128)(2,1)S(1)} %shear_back.1), channel_id=1, replica_groups=mesh['ang'=8,'strip'=32] {'ang'}, dimensions={0} | all-to-all | bytes 524288 | tf_op jit(solution)/shard_map/all_to_all | solution.py:286
  80.7 0.9 %convert.1 = f32[1,2,128,512]{3,2,1,0:T(8,128)} convert(bf16[1,2,128,512]{3,2,1,0:T(8,128)(2,1)S(1)} %bitcast.12) | non-fusion elementwise | flops 131072 | bytes 786432 | tf_op jit(solution)/shard_map/convert_element_type | solution.py:297
Async XLA Ops:
  0.0 39.2 %copy-start.2 = (bf16[512,512]{1,0:T(8,128)(2,1)S(1)}, bf16[512,512]{1,0:T(8,128)(2,1)}, u32[]{:S(2)}) copy-start(bf16[512,512]{1,0:T(8,128)(2,1)} %constant.10.clone.fwd_ref) | copy-start | bytes 1572868
  14.9 24.3 %copy-start = (bf16[1,4,256,256]{3,2,1,0:T(8,128)(2,1)S(1)}, bf16[1,4,256,256]{3,2,1,0:T(8,128)(2,1)}, u32[]{:S(2)}) copy-start(bf16[1,4,256,256]{3,2,1,0:T(8,128)(2,1)} %param.17) | copy-start | bytes 1572868
  14.9 24.3 %copy-start.1 = (bf16[512,512]{1,0:T(8,128)(2,1)S(1)}, bf16[512,512]{1,0:T(8,128)(2,1)}, u32[]{:S(2)}) copy-start(bf16[512,512]{1,0:T(8,128)(2,1)} %constant.11.clone.inv_ref) | copy-start | bytes 1572868
  29.4 9.8 %collective-permute-start.1 = (bf16[2,128,512]{2,1,0:T(8,128)(2,1)S(1)}, bf16[2,128,512]{2,1,0:T(8,128)(2,1)S(1)}, u32[]{:S(2)}, u32[]{:S(2)}) collective-permute-start(bf16[2,128,512]{2,1,0:T(8,128)(2,1)S(1)} %bitcast.7), channel_id=1, source_target_pairs={{1,2},{2,1},{3,4},{4,3},{5,6},{6,5},{7,8},{8,7},{9,10},{10,9},{11,... | collective-permute-start | bytes 786440 | tf_op jit(solution)/shard_map/ppermute | solution.py:277
  35.1 4.1 %collective-permute-start = (bf16[2,128,512]{2,1,0:T(8,128)(2,1)S(1)}, bf16[2,128,512]{2,1,0:T(8,128)(2,1)S(1)}, u32[]{:S(2)}, u32[]{:S(2)}) collective-permute-start(bf16[2,128,512]{2,1,0:T(8,128)(2,1)S(1)} %bitcast.8), channel_id=1, source_target_pairs={{0,1},{1,0},{2,3},{3,2},{4,5},{5,4},{6,7},{7,6},{8,9},{9,8},{10,11... | collective-permute-start | bytes 786440 | tf_op jit(solution)/shard_map/ppermute | solution.py:277
  43.2 5.5 %collective-permute-start.2 = (bf16[2,128,512]{2,1,0:T(8,128)(2,1)S(1)}, bf16[2,128,512]{2,1,0:T(8,128)(2,1)S(1)}, u32[]{:S(2)}, u32[]{:S(2)}) collective-permute-start(bf16[2,128,512]{2,1,0:T(8,128)(2,1)S(1)} %get-tuple-element.9), channel_id=1, source_target_pairs={{0,1},{1,0},{2,3},{3,2},{4,5},{5,4},{6,7},{7,6},{8,9},{9,8},{10,11... | collective-permute-start | bytes 786440 | tf_op jit(solution)/shard_map/ppermute | solution.py:277
  44.3 9.8 %collective-permute-start.3 = (bf16[2,128,512]{2,1,0:T(8,128)(2,1)S(1)}, bf16[2,128,512]{2,1,0:T(8,128)(2,1)S(1)}, u32[]{:S(2)}, u32[]{:S(2)}) collective-permute-start(bf16[2,128,512]{2,1,0:T(8,128)(2,1)S(1)} %get-tuple-element.10), channel_id=1, source_target_pairs={{1,2},{2,1},{3,4},{4,3},{5,6},{6,5},{7,8},{8,7},{9,10},{10,9},{11,... | collective-permute-start | bytes 786440 | tf_op jit(solution)/shard_map/ppermute | solution.py:277
where the time goes:
time: 82.2 us; the launch traced here: 81.6 us
  blocking collectives  49.7 us (60%)
  starting transfers between devices  11.2 us (14%)
  Pallas kernels  10.2 us (12%)
  waiting for transfers between devices  8.78 us (11%)
  other arithmetic  0.96 us (1%)
    all_to_all x4, blocking collectives, exchange(): return lax.all_to_all(x, 'ang', 0, 0, tiled=True)  49.7 us
    ppermute x4, starting transfers between devices, swap(): return lax.ppermute(x, 'strip', route)  11.2 us
    ppermute x4, waiting for transfers between devices, swap(): return lax.ppermute(x, 'strip', route)  8.78 us
    pallas_call x2, Pallas kernels, shear(): pl.pallas_call(functools.partial(shear_body, sign), out_shape=jax.ShapeDt...  6.21 us
    pallas_call x1, Pallas kernels, frames(): pl.pallas_call(frames_body, out_shape=(jax.ShapeDtypeStruct(own.shape, jn...  3.98 us
  transfers between devices with their start and end apart: 4, of which 2 were waited for; matrix products, arithmetic and copies ran while one was open for 0% of the time, Pallas kernels for 0%

commit v1 on v0

--- a/solution.py
+++ b/solution.py
@@ -38,7 +38,8 @@
 
 
 def shear_body(sign, taps_hbm, offsets_hbm, x_ref, o_ref, taps_ref, offsets_ref, ready, copies):
-    count, rows, width = x_ref.shape
+    count = taps_ref.shape[1]
+    rows, width = x_ref.shape[1:]
     tiles = width // LANES + 1
     ntaps = taps_ref.shape[0]
     left = MAXSHIFT if sign > 0 else MAXSHIFT + ntaps - 1
@@ -49,6 +50,8 @@
 
     def lay_out(s, _):
         value = x_ref[s].astype(jnp.float32)
+        for again in range(1, x_ref.shape[0] // count):
+            value = value + x_ref[s + again * count].astype(jnp.float32)
         value = jnp.concatenate([value, jnp.zeros((rows, LANES), jnp.float32)], axis=1)
         for k in range(ntaps):
             moved = pltpu.roll(value, left - k, axis=1)
@@ -77,18 +80,21 @@
             for j in range(tiles - 1):
                 total[j] = total[j] + jnp.where(keep, turned[j], turned[j + 1])
         for j in range(tiles - 1):
-            o_ref[d, :, pl.ds(j * LANES, LANES)] = total[j].astype(o_ref.dtype)
+            out = total[j].astype(o_ref.dtype)
+            for again in range(o_ref.shape[0] // count):
+                o_ref[d + again * count, :, pl.ds(j * LANES, LANES)] = out
         return 0
 
     lax.fori_loop(0, count, one, 0)
 
 
-def shear(x, taps, offsets, sign):
-    count, rows, width = x.shape
+def shear(x, taps, offsets, sign, copies):
+    rows, width = x.shape[1:]
+    count = taps.shape[1]
     tiles = width // LANES + 1
     return pl.pallas_call(
         functools.partial(shear_body, sign),
-        out_shape=jax.ShapeDtypeStruct(x.shape, jnp.bfloat16),
+        out_shape=jax.ShapeDtypeStruct((copies * count, rows, width), jnp.bfloat16),
         in_specs=[
             pl.BlockSpec(memory_space=pltpu.HBM),
             pl.BlockSpec(memory_space=pltpu.HBM),
@@ -107,35 +113,39 @@
 
 
 def frames_body(
-    odd_ref, counts_ref, rows_hbm, columns_hbm, own_ref, near_ref, far_ref, probe_hbm, amp_ref, fwd_ref, inv_ref,
-    mid_ref, to_near_ref, to_far_ref,
-    ready, rows_ref, columns_ref, probe_ref, ext, placed,
+    place_ref, counts_ref, rows_hbm, columns_hbm, pair_ref, near_ref, probe_hbm, fwd_hbm, inv_hbm, amp_hbm,
+    mid_ref, to_near_ref, send_ref,
+    ready, rows_ref, columns_ref, probe_ref, fwd_ref, inv_ref, amp_ref, ext, placed,
     column_a, column_b, side_a, side_b, wave_a,
 ):
     length = probe_ref.shape[1]
-    strip = own_ref.shape[1]
-    width = own_ref.shape[2]
-    gets = [
-        pltpu.make_async_copy(src, dst, ready.at[i])
-        for i, (src, dst) in enumerate(
-            [(rows_hbm, rows_ref), (columns_hbm, columns_ref), (probe_hbm, probe_ref)]
-        )
+    strip, width = near_ref.shape[1:]
+    pairs = [
+        (rows_hbm, rows_ref),
+        (columns_hbm, columns_ref),
+        (probe_hbm, probe_ref),
+        (fwd_hbm, fwd_ref),
+        (inv_hbm, inv_ref),
+        (amp_hbm, amp_ref),
     ]
+    gets = [pltpu.make_async_copy(src, dst, ready.at[i]) for i, (src, dst) in enumerate(pairs)]
     for get in gets:
         get.start()
-    odd = odd_ref[0]
+    odd = place_ref[0]
+    has_far = place_ref[1] > 0
     near_row = pl.multiple_of((1 - odd) * 2 * strip, strip)
     far_row = pl.multiple_of(odd * 2 * strip, strip)
     tiles = width // LANES
     for p in range(2):
         for j in range(tiles):
             tile = pl.ds(j * LANES, LANES)
-            ext[p, j, pl.ds(strip, strip), :] = own_ref[p, :, tile].astype(jnp.float32)
+            ext[p, j, pl.ds(strip, strip), :] = pair_ref[1 - odd, p, :, tile].astype(jnp.float32)
             ext[p, j, pl.ds(near_row, strip), :] = near_ref[p, :, tile].astype(jnp.float32)
-            ext[p, j, pl.ds(far_row, strip), :] = far_ref[p, :, tile].astype(jnp.float32)
+            far = pair_ref[odd, p, :, tile].astype(jnp.float32)
+            ext[p, j, pl.ds(far_row, strip), :] = jnp.where(has_far, far, 0.0)
     placed[...] = jnp.zeros_like(placed)
     wave_a[...] = jnp.zeros_like(wave_a)
-    for get in gets:
+    for get in gets[:3]:
         get.wait()
     part = 16
     lane = lane_index((part, LANES))
@@ -222,6 +232,8 @@
         return 0
 
     cut(0, column_a)
+    for get in gets[3:]:
+        get.wait()
     lax.fori_loop(0, count, one_frame, 0)
     add(count - 1, wave_a)
     for p in range(2):
@@ -229,29 +241,34 @@
             tile = pl.ds(j * LANES, LANES)
             mid_ref[p, :, tile] = placed[p, j, pl.ds(strip, strip), :]
             to_near_ref[p, :, tile] = placed[p, j, pl.ds(near_row, strip), :].astype(to_near_ref.dtype)
-            to_far_ref[p, :, tile] = placed[p, j, pl.ds(far_row, strip), :].astype(to_far_ref.dtype)
-
-
-def frames(odd, rows, columns, counts, own, near, far, probe, amplitudes):
+            far = jnp.where(has_far, placed[p, j, pl.ds(far_row, strip), :], 0.0)
+            send_ref[odd, p, :, tile] = far.astype(send_ref.dtype)
+
+
+def frames(place, counts, rows, columns, pair, near, probe, amplitudes):
     length = probe.shape[1]
-    parts, strip, width = own.shape
+    parts, strip, width = near.shape
     fwd, inv = (jnp.asarray(m) for m in dft_blocks(length))
+    smem = pl.BlockSpec(memory_space=SMEM)
     hbm = pl.BlockSpec(memory_space=pltpu.HBM)
     vmem = pl.BlockSpec(memory_space=VMEM)
     return pl.pallas_call(
         frames_body,
         out_shape=(
-            jax.ShapeDtypeStruct(own.shape, jnp.float32),
-            jax.ShapeDtypeStruct(own.shape, jnp.bfloat16),
-            jax.ShapeDtypeStruct(own.shape, jnp.bfloat16),
+            jax.ShapeDtypeStruct(near.shape, jnp.float32),
+            jax.ShapeDtypeStruct(near.shape, jnp.bfloat16),
+            jax.ShapeDtypeStruct(pair.shape, jnp.bfloat16),
         ),
-        in_specs=[pl.BlockSpec(memory_space=SMEM)] * 2 + [hbm] * 2 + [vmem] * 3 + [hbm] + [vmem] * 3,
+        in_specs=[smem] * 2 + [hbm] * 2 + [vmem] * 2 + [hbm] * 4,
         out_specs=(vmem,) * 3,
         scratch_shapes=[
-            pltpu.SemaphoreType.DMA((3,)),
+            pltpu.SemaphoreType.DMA((6,)),
             SMEM(rows.shape, rows.dtype),
             SMEM(columns.shape, columns.dtype),
             VMEM(probe.shape, probe.dtype),
+            VMEM(fwd.shape, fwd.dtype),
+            VMEM(inv.shape, inv.dtype),
+            VMEM(amplitudes.shape, amplitudes.dtype),
             VMEM((parts, width // LANES + 1, 3 * strip, LANES), jnp.float32),
             VMEM((parts, width // LANES + 1, 3 * strip, LANES), jnp.float32),
             VMEM((2 * length, length), jnp.bfloat16),
@@ -262,7 +279,7 @@
         ],
         compiler_params=pltpu.CompilerParams(vmem_limit_bytes=32 << 20),
         name="frames",
-    )(odd, counts, in_hbm(rows), in_hbm(columns), own, near, far, in_hbm(probe), amplitudes, fwd, inv)
+    )(place, counts, in_hbm(rows), in_hbm(columns), pair, near, in_hbm(probe), in_hbm(fwd), in_hbm(inv), in_hbm(amplitudes))
 
 
 def per_device(slab, taps, offsets, probe, scan_rows, scan_columns, counts, amplitudes):
@@ -271,29 +288,30 @@
     strips = lax.axis_size("strip")
     block = parts * rows // angles
     me = lax.axis_index("strip")
-
-    def swap(x, partner):
-        route = [(s, partner(s)) for s in range(strips) if 0 <= partner(s) < strips]
-        return lax.ppermute(x, "strip", route)
-
-    def near(x):
-        return swap(x, lambda s: s ^ 1)
-
-    def far(x):
-        return swap(x, lambda s: s + 1 if s % 2 else s - 1)
+    odd = (me & 1).astype(jnp.int32)
+    has_far = ((me > 0) & (me < strips - 1)).astype(jnp.int32)
+    groups = [
+        [a * strips + s % strips for s in (first, first + 1) for a in range(angles)] for first in range(1, strips, 2)
+    ]
+
+    def swap(x):
+        return lax.ppermute(x, "strip", [(s, s ^ 1) for s in range(strips)])
 
     def exchange(x):
         return lax.all_to_all(x, "ang", 0, 0, tiled=True)
 
+    def pair_exchange(x):
+        return lax.all_to_all(x, ("ang", "strip"), 0, 0, axis_index_groups=groups, tiled=True)
+
     mixed = exchange(slab.reshape(angles, block, width))
-    projection = exchange(shear(mixed, taps, offsets, 1)).reshape(parts, rows, width)
-    odd = (me & 1).astype(jnp.int32).reshape(1)
-    mid, to_near, to_far = frames(
-        odd, scan_rows, scan_columns, counts, projection, near(projection), far(projection), probe, amplitudes[0]
-    )
-    image = mid + near(to_near).astype(jnp.float32) + far(to_far).astype(jnp.float32)
-    mixed = exchange(image.astype(jnp.bfloat16).reshape(angles, block, width))
-    result = exchange(shear(mixed, taps, offsets, -1))
+    pair = pair_exchange(shear(mixed, taps, offsets, 1, 2)).reshape(2, parts, rows, width)
+    near = swap(lax.dynamic_index_in_dim(pair, 1 - odd, 0, keepdims=False))
+    place = jnp.stack([odd, has_far])
+    mid, to_near, send = frames(place, counts, scan_rows, scan_columns, pair, near, probe, amplitudes[0])
+    own = (mid + swap(to_near).astype(jnp.float32)).astype(jnp.bfloat16)
+    send = lax.dynamic_update_index_in_dim(send, own, 1 - odd, 0)
+    mixed = pair_exchange(send.reshape(2 * angles, block, width))
+    result = exchange(shear(mixed, taps, offsets, -1, 1))
     return result.reshape(1, parts, rows, width).astype(jnp.float32)
 
 

time: 82.2 us -> 78.1 us (0.950)
  blocking collectives: 49.7 us -> 41.7 us
  Pallas kernels: 10.2 us -> 14.3 us
  starting transfers between devices: 11.2 us -> 8.34 us
  waiting for transfers between devices: 8.78 us -> 10.9 us
    all_to_all x4 -> x2, blocking collectives: 49.7 us -> 26.5 us  [exchange(): return lax.all_to_all(x, 'ang', 0, 0, tiled=True)]
    all_to_all x0 -> x1, blocking collectives: none -> 15.2 us  [pair_exchange(): lax.all_to_all(x, ('ang', 'strip'), 0, 0, axis_index_groups=groups, tiled...]
    ppermute x4 -> x2, starting transfers between devices: 11.2 us -> 0.19 us  [swap(): return lax.ppermute(x, 'strip', [(s, s ^ 1) for s in range(strips)])]
    all_to_all x0 -> x1, waiting for transfers between devices: none -> 8.58 us  [pair_exchange(): lax.all_to_all(x, ('ang', 'strip'), 0, 0, axis_index_groups=groups, tiled...]
    all_to_all x0 -> x1, starting transfers between devices: none -> 8.16 us  [pair_exchange(): lax.all_to_all(x, ('ang', 'strip'), 0, 0, axis_index_groups=groups, tiled...]
    ppermute x4 -> x2, waiting for transfers between devices: 8.78 us -> 2.31 us  [swap(): return lax.ppermute(x, 'strip', [(s, s ^ 1) for s in range(strips)])]
    pallas_call x1, Pallas kernels: 3.98 us -> 7.27 us  [frames(): pl.pallas_call(frames_body, out_shape=(jax.ShapeDtypeStruct(near.shape, j...]
    pallas_call x2, Pallas kernels: 6.21 us -> 7.05 us  [shear(): pl.pallas_call(functools.partial(shear_body, sign), out_shape=jax.ShapeDt...]
  transfers between devices with their start and end apart: 4 -> 3, of which waited for: 2 -> 3; matrix products, arithmetic and copies ran while one was open for 0% -> 0% of each run, Pallas kernels for 0% -> 0%
where the time goes in v1:
time: 78.1 us; the launch traced here: 77 us
  blocking collectives  41.7 us (53%)
  Pallas kernels  14.3 us (18%)
  waiting for transfers between devices  10.9 us (14%)
  starting transfers between devices  8.34 us (11%)
  other arithmetic  1 us (1%)
    all_to_all x2, blocking collectives, exchange(): return lax.all_to_all(x, 'ang', 0, 0, tiled=True)  26.5 us
    all_to_all x1, blocking collectives, pair_exchange(): lax.all_to_all(x, ('ang', 'strip'), 0, 0, axis_index_groups=groups, tiled...  15.2 us
    all_to_all x1, waiting for transfers between devices, pair_exchange(): lax.all_to_all(x, ('ang', 'strip'), 0, 0, axis_index_groups=groups, tiled...  8.58 us
    all_to_all x1, starting transfers between devices, pair_exchange(): lax.all_to_all(x, ('ang', 'strip'), 0, 0, axis_index_groups=groups, tiled...  8.16 us
    pallas_call x1, Pallas kernels, frames(): pl.pallas_call(frames_body, out_shape=(jax.ShapeDtypeStruct(near.shape, j...  7.27 us
    pallas_call x2, Pallas kernels, shear(): pl.pallas_call(functools.partial(shear_body, sign), out_shape=jax.ShapeDt...  7.05 us
    ppermute x2, waiting for transfers between devices, swap(): return lax.ppermute(x, 'strip', [(s, s ^ 1) for s in range(strips)])  2.31 us
  transfers between devices with their start and end apart: 3, of which 3 were waited for; matrix products, arithmetic and copies ran while one was open for 0% of the time, Pallas kernels for 0%

profile of v1, /device:TPU:2, one launch (start us, length us, event | category | flops | bytes accessed | tf_op | source)
XLA Modules:
  0.0 77.0 jit_solution(10980988734603315222)
XLA Ops:
  0.0 14.8 %all_to_all.20.x_ref = bf16[8,32,512]{2,1,0:T(8,128)(2,1)S(1)} all-to-all(bf16[8,32,512]{2,1,0:T(8,128)(2,1)} %bitcast.19), channel_id=1, replica_groups=mesh['ang'=8,'strip'=32] {'ang'}, dimensions={0} | all-to-all | bytes 524288 | tf_op jit(solution)/shard_map/all_to_all | solution.py:301
  14.8 3.8 %shear_forward.1 = bf16[16,32,512]{2,1,0:T(8,128)(2,1)} custom-call(f32[4,8,8]{2,1,0:T(8,128)} %taps_hbm.3, s32[8,8]{1,0:T(8,128)} %offsets_hbm.3, bf16[8,32,512]{2,1,0:T(8,128)(2,1)S(1)} %all_to_all.20.x_ref), custom_call_target="tpu_custom_call" | custom-call | tf_op jit(solution)/shard_map/shear_forward/pallas_call | solution.py:95
  18.6 8.2 %all-to-all-start.1 = ((bf16[16,32,512]{2,1,0:T(8,128)(2,1)}), bf16[16,32,512]{2,1,0:T(8,128)(2,1)S(1)}, u32[]{:S(2)}, u32[]{:S(2)}) async-start(bf16[16,32,512]{2,1,0:T(8,128)(2,1)} %shear_forward.1), calls=%async_computation.1 | async-start | bytes 1048576 | tf_op jit(solution)/shard_map/all_to_all | solution.py:304
  26.8 8.6 %all-to-all-done.1 = bf16[16,32,512]{2,1,0:T(8,128)(2,1)S(1)} async-done(((bf16[16,32,512]{2,1,0:T(8,128)(2,1)}), bf16[16,32,512]{2,1,0:T(8,128)(2,1)S(1)}, u32[]{:S(2)}, u32[]{:S(2)}) %all-to-all-start.1) | async-done | bytes 524320 | tf_op jit(solution)/shard_map/all_to_all | solution.py:304
  35.4 0.1 collective-permute-start
  36.1 0.1 pad_add_fusion.place_ref
  36.2 0.8 %collective-permute-done.near_ref = bf16[2,128,512]{2,1,0:T(8,128)(2,1)S(1)} collective-permute-done((bf16[2,128,512]{2,1,0:T(8,128)(2,1)S(1)}, bf16[2,128,512]{2,1,0:T(8,128)(2,1)S(1)}, u32[]{:S(2)}, u32[]{:S(2)}) %collective-permute-start) | collective-permute-done | bytes 262176 | tf_op jit(solution)/shard_map/ppermute | solution.py:298
  37.0 7.3 %frames.1 = (f32[2,128,512]{2,1,0:T(8,128)S(1)}, bf16[2,128,512]{2,1,0:T(8,128)(2,1)S(1)}, bf16[2,2,128,512]{3,2,1,0:T(8,128)(2,1)S(1)}) custom-call(s32[2]{0:T(128)S(1)} %pad_add_fusion.place_ref, s32[1,1]{1,0:T(1,128)S(6)} %copy.12.counts_ref, s32[1,4]{1,0:T(1,128)} %rows_hbm.1, s32[1,4]{1,0:T(1,128)} %columns_hbm.1, ...), custom_call_target="tpu_custom_call" | custom-call | tf_op jit(solution)/shard_map/frames/pallas_call | solution.py:255
  44.3 0.1 collective-permute-start.1
  44.4 1.5 %collective-permute-done.1 = bf16[2,128,512]{2,1,0:T(8,128)(2,1)S(1)} collective-permute-done((bf16[2,128,512]{2,1,0:T(8,128)(2,1)S(1)}, bf16[2,128,512]{2,1,0:T(8,128)(2,1)S(1)}, u32[]{:S(2)}, u32[]{:S(2)}) %collective-permute-start.1) | collective-permute-done | bytes 262176 | tf_op jit(solution)/shard_map/ppermute | solution.py:298
  45.9 0.1 fusion.1
  46.0 15.2 %all_to_all.21.x_ref = bf16[16,32,512]{2,1,0:T(8,128)(2,1)S(1)} all-to-all(bf16[16,32,512]{2,1,0:T(8,128)(2,1)S(1)} %bitcast.16), channel_id=1, replica_groups={{1,33,65,97,129,161,193,225,2,34,66,98,130,162,194,226},{3,35,67,99,131..., dimensions={0} | all-to-all | bytes 1048576 | tf_op jit(solution)/shard_map/all_to_all | solution.py:304
  61.1 3.2 %shear_back.1 = bf16[8,32,512]{2,1,0:T(8,128)(2,1)S(1)} custom-call(f32[4,8,8]{2,1,0:T(8,128)} %taps_hbm.3, s32[8,8]{1,0:T(8,128)} %offsets_hbm.3, bf16[16,32,512]{2,1,0:T(8,128)(2,1)S(1)} %all_to_all.21.x_ref), custom_call_target="tpu_custom_call" | custom-call | tf_op jit(solution)/shard_map/shear_back/pallas_call | solution.py:95
  64.4 11.8 %all_to_all.22 = bf16[8,32,512]{2,1,0:T(8,128)(2,1)S(1)} all-to-all(bf16[8,32,512]{2,1,0:T(8,128)(2,1)S(1)} %shear_back.1), channel_id=1, replica_groups=mesh['ang'=8,'strip'=32] {'ang'}, dimensions={0} | all-to-all | bytes 524288 | tf_op jit(solution)/shard_map/all_to_all | solution.py:301
  76.1 0.9 %convert.2 = f32[1,2,128,512]{3,2,1,0:T(8,128)} convert(bf16[1,2,128,512]{3,2,1,0:T(8,128)(2,1)S(1)} %bitcast.17) | non-fusion elementwise | flops 131072 | bytes 786432 | tf_op jit(solution)/shard_map/convert_element_type | solution.py:315
  (1 shorter events, 0.0 us)
Async XLA Ops:
  18.6 16.7 %all-to-all-start.1 = ((bf16[16,32,512]{2,1,0:T(8,128)(2,1)}), bf16[16,32,512]{2,1,0:T(8,128)(2,1)S(1)}, u32[]{:S(2)}, u32[]{:S(2)}) async-start(bf16[16,32,512]{2,1,0:T(8,128)(2,1)} %shear_forward.1), calls=%async_computation.1 | async-start | bytes 1048576 | tf_op jit(solution)/shard_map/all_to_all | solution.py:304
  35.4 1.6 %collective-permute-start = (bf16[2,128,512]{2,1,0:T(8,128)(2,1)S(1)}, bf16[2,128,512]{2,1,0:T(8,128)(2,1)S(1)}, u32[]{:S(2)}, u32[]{:S(2)}) collective-permute-start(bf16[2,128,512]{2,1,0:T(8,128)(2,1)S(1)} %dynamic-slice_bitcast_fusion), channel_id=1, source_target_pairs={{0,1},{1,0},{2,3},{3,2},{4,5},{5,4},{6,7},{7,6},{8,9},{9,8},{10,11... | collective-permute-start | bytes 786440 | tf_op jit(solution)/shard_map/ppermute | solution.py:298
  44.3 1.6 %collective-permute-start.1 = (bf16[2,128,512]{2,1,0:T(8,128)(2,1)S(1)}, bf16[2,128,512]{2,1,0:T(8,128)(2,1)S(1)}, u32[]{:S(2)}, u32[]{:S(2)}) collective-permute-start(bf16[2,128,512]{2,1,0:T(8,128)(2,1)S(1)} %get-tuple-element.10), channel_id=1, source_target_pairs={{0,1},{1,0},{2,3},{3,2},{4,5},{5,4},{6,7},{7,6},{8,9},{9,8},{10,11... | collective-permute-start | bytes 786440 | tf_op jit(solution)/shard_map/ppermute | solution.py:298

commit v2 on v1

--- a/solution.py
+++ b/solution.py
@@ -37,7 +37,8 @@
     return lax.broadcasted_iota(jnp.int32, shape, len(shape) - 1)
 
 
-def shear_body(sign, taps_hbm, offsets_hbm, x_ref, o_ref, taps_ref, offsets_ref, ready, copies):
+def shear_body(sign, ahead, taps_hbm, offsets_hbm, x_ref, *refs):
+    o_ref, taps_ref, offsets_ref, ready, copies = refs[ahead:]
     count = taps_ref.shape[1]
     rows, width = x_ref.shape[1:]
     tiles = width // LANES + 1
@@ -88,18 +89,19 @@
     lax.fori_loop(0, count, one, 0)
 
 
-def shear(x, taps, offsets, sign, copies):
+def shear(x, taps, offsets, sign, copies, *ahead):
     rows, width = x.shape[1:]
     count = taps.shape[1]
     tiles = width // LANES + 1
     return pl.pallas_call(
-        functools.partial(shear_body, sign),
+        functools.partial(shear_body, sign, len(ahead)),
         out_shape=jax.ShapeDtypeStruct((copies * count, rows, width), jnp.bfloat16),
         in_specs=[
             pl.BlockSpec(memory_space=pltpu.HBM),
             pl.BlockSpec(memory_space=pltpu.HBM),
             pl.BlockSpec(memory_space=VMEM),
-        ],
+        ]
+        + [pl.BlockSpec(memory_space=SMEM)] * len(ahead),
         out_specs=pl.BlockSpec(memory_space=VMEM),
         scratch_shapes=[
             SMEM(taps.shape, taps.dtype),
@@ -109,13 +111,13 @@
         ],
         compiler_params=pltpu.CompilerParams(vmem_limit_bytes=16 << 20),
         name="shear_forward" if sign > 0 else "shear_back",
-    )(in_hbm(taps), in_hbm(offsets), x)
+    )(in_hbm(taps), in_hbm(offsets), x, *ahead)
 
 
 def frames_body(
-    place_ref, counts_ref, rows_hbm, columns_hbm, pair_ref, near_ref, probe_hbm, fwd_hbm, inv_hbm, amp_hbm,
+    strips, strip_ref, counts_ref, rows_hbm, columns_hbm, pair_ref, near_ref, probe_hbm, fwd_ref, inv_ref, amp_ref,
     mid_ref, to_near_ref, send_ref,
-    ready, rows_ref, columns_ref, probe_ref, fwd_ref, inv_ref, amp_ref, ext, placed,
+    ready, rows_ref, columns_ref, probe_ref, ext, placed,
     column_a, column_b, side_a, side_b, wave_a,
 ):
     length = probe_ref.shape[1]
@@ -124,15 +126,13 @@
         (rows_hbm, rows_ref),
         (columns_hbm, columns_ref),
         (probe_hbm, probe_ref),
-        (fwd_hbm, fwd_ref),
-        (inv_hbm, inv_ref),
-        (amp_hbm, amp_ref),
     ]
     gets = [pltpu.make_async_copy(src, dst, ready.at[i]) for i, (src, dst) in enumerate(pairs)]
     for get in gets:
         get.start()
-    odd = place_ref[0]
-    has_far = place_ref[1] > 0
+    me = strip_ref[0]
+    odd = me & 1
+    has_far = (me > 0) & (me < strips - 1)
     near_row = pl.multiple_of((1 - odd) * 2 * strip, strip)
     far_row = pl.multiple_of(odd * 2 * strip, strip)
     tiles = width // LANES
@@ -145,7 +145,7 @@
             ext[p, j, pl.ds(far_row, strip), :] = jnp.where(has_far, far, 0.0)
     placed[...] = jnp.zeros_like(placed)
     wave_a[...] = jnp.zeros_like(wave_a)
-    for get in gets[:3]:
+    for get in gets:
         get.wait()
     part = 16
     lane = lane_index((part, LANES))
@@ -232,8 +232,6 @@
         return 0
 
     cut(0, column_a)
-    for get in gets[3:]:
-        get.wait()
     lax.fori_loop(0, count, one_frame, 0)
     add(count - 1, wave_a)
     for p in range(2):
@@ -245,7 +243,7 @@
             send_ref[odd, p, :, tile] = far.astype(send_ref.dtype)
 
 
-def frames(place, counts, rows, columns, pair, near, probe, amplitudes):
+def frames(me, strips, counts, rows, columns, pair, near, probe, amplitudes):
     length = probe.shape[1]
     parts, strip, width = near.shape
     fwd, inv = (jnp.asarray(m) for m in dft_blocks(length))
@@ -253,22 +251,19 @@
     hbm = pl.BlockSpec(memory_space=pltpu.HBM)
     vmem = pl.BlockSpec(memory_space=VMEM)
     return pl.pallas_call(
-        frames_body,
+        functools.partial(frames_body, strips),
         out_shape=(
             jax.ShapeDtypeStruct(near.shape, jnp.float32),
             jax.ShapeDtypeStruct(near.shape, jnp.bfloat16),
             jax.ShapeDtypeStruct(pair.shape, jnp.bfloat16),
         ),
-        in_specs=[smem] * 2 + [hbm] * 2 + [vmem] * 2 + [hbm] * 4,
+        in_specs=[smem] * 2 + [hbm] * 2 + [vmem] * 2 + [hbm] + [vmem] * 3,
         out_specs=(vmem,) * 3,
         scratch_shapes=[
-            pltpu.SemaphoreType.DMA((6,)),
+            pltpu.SemaphoreType.DMA((3,)),
             SMEM(rows.shape, rows.dtype),
             SMEM(columns.shape, columns.dtype),
             VMEM(probe.shape, probe.dtype),
-            VMEM(fwd.shape, fwd.dtype),
-            VMEM(inv.shape, inv.dtype),
-            VMEM(amplitudes.shape, amplitudes.dtype),
             VMEM((parts, width // LANES + 1, 3 * strip, LANES), jnp.float32),
             VMEM((parts, width // LANES + 1, 3 * strip, LANES), jnp.float32),
             VMEM((2 * length, length), jnp.bfloat16),
@@ -279,7 +274,7 @@
         ],
         compiler_params=pltpu.CompilerParams(vmem_limit_bytes=32 << 20),
         name="frames",
-    )(place, counts, in_hbm(rows), in_hbm(columns), pair, near, in_hbm(probe), in_hbm(fwd), in_hbm(inv), in_hbm(amplitudes))
+    )(me, counts, in_hbm(rows), in_hbm(columns), pair, near, in_hbm(probe), fwd, inv, amplitudes)
 
 
 def per_device(slab, taps, offsets, probe, scan_rows, scan_columns, counts, amplitudes):
@@ -288,8 +283,8 @@
     strips = lax.axis_size("strip")
     block = parts * rows // angles
     me = lax.axis_index("strip")
-    odd = (me & 1).astype(jnp.int32)
-    has_far = ((me > 0) & (me < strips - 1)).astype(jnp.int32)
+    own_half = (me.astype(jnp.uint32) & 1) ^ 1
+    place, half = me.astype(jnp.int32).reshape(1), own_half.astype(jnp.int32).reshape(1)
     groups = [
         [a * strips + s % strips for s in (first, first + 1) for a in range(angles)] for first in range(1, strips, 2)
     ]
@@ -304,12 +299,11 @@
         return lax.all_to_all(x, ("ang", "strip"), 0, 0, axis_index_groups=groups, tiled=True)
 
     mixed = exchange(slab.reshape(angles, block, width))
-    pair = pair_exchange(shear(mixed, taps, offsets, 1, 2)).reshape(2, parts, rows, width)
-    near = swap(lax.dynamic_index_in_dim(pair, 1 - odd, 0, keepdims=False))
-    place = jnp.stack([odd, has_far])
-    mid, to_near, send = frames(place, counts, scan_rows, scan_columns, pair, near, probe, amplitudes[0])
+    pair = pair_exchange(shear(mixed, taps, offsets, 1, 2, place, half)).reshape(2, parts, rows, width)
+    near = swap(lax.dynamic_index_in_dim(pair, own_half, 0, keepdims=False))
+    mid, to_near, send = frames(place, strips, counts, scan_rows, scan_columns, pair, near, probe, amplitudes[0])
     own = (mid + swap(to_near).astype(jnp.float32)).astype(jnp.bfloat16)
-    send = lax.dynamic_update_index_in_dim(send, own, 1 - odd, 0)
+    send = lax.dynamic_update_index_in_dim(send, own, own_half, 0)
     mixed = pair_exchange(send.reshape(2 * angles, block, width))
     result = exchange(shear(mixed, taps, offsets, -1, 1))
     return result.reshape(1, parts, rows, width).astype(jnp.float32)

time: 78.1 us -> 76.8 us (0.983)
  blocking collectives: 41.7 us -> 44.1 us
  starting transfers between devices: 8.34 us -> 6.22 us
  Pallas kernels: 14.3 us -> 12.7 us
    all_to_all x1 -> x2, blocking collectives: 15.2 us -> 32.1 us  [pair_exchange(): lax.all_to_all(x, ('ang', 'strip'), 0, 0, axis_index_groups=groups, tiled...]
    all_to_all x2 -> x1, blocking collectives: 26.5 us -> 12 us  [exchange(): return lax.all_to_all(x, 'ang', 0, 0, tiled=True)]
    all_to_all x1, starting transfers between devices: 8.16 us -> 6.03 us  [exchange(): return lax.all_to_all(x, 'ang', 0, 0, tiled=True)]
    pallas_call x3, Pallas kernels: 14.3 us -> 12.7 us  [the longest x1 6.46 us: frames(): pl.pallas_call(functools.partial(frames_body, strips), out_shape=(jax.Sha...]
where the time goes in v2:
time: 76.8 us; the launch traced here: 75.8 us
  blocking collectives  44.1 us (57%)
  Pallas kernels  12.7 us (17%)
  waiting for transfers between devices  11.1 us (14%)
  starting transfers between devices  6.22 us (8%)
  other arithmetic  0.92 us (1%)
    all_to_all x2, blocking collectives, pair_exchange(): lax.all_to_all(x, ('ang', 'strip'), 0, 0, axis_index_groups=groups, tiled...  32.1 us
    all_to_all x1, blocking collectives, exchange(): return lax.all_to_all(x, 'ang', 0, 0, tiled=True)  12 us
    all_to_all x1, waiting for transfers between devices, exchange(): return lax.all_to_all(x, 'ang', 0, 0, tiled=True)  8.73 us
    pallas_call x1, Pallas kernels, frames(): pl.pallas_call(functools.partial(frames_body, strips), out_shape=(jax.Sha...  6.46 us
    pallas_call x2, Pallas kernels, shear(): pl.pallas_call(functools.partial(shear_body, sign, len(ahead)), out_shape...  6.25 us
    all_to_all x1, starting transfers between devices, exchange(): return lax.all_to_all(x, 'ang', 0, 0, tiled=True)  6.03 us
    ppermute x2, waiting for transfers between devices, swap(): return lax.ppermute(x, 'strip', [(s, s ^ 1) for s in range(strips)])  2.36 us
  transfers between devices with their start and end apart: 3, of which 3 were waited for; matrix products, arithmetic and copies ran while one was open for 0% of the time, Pallas kernels for 0%

profile of v2, /device:TPU:2, one launch (start us, length us, event | category | flops | bytes accessed | tf_op | source)
XLA Modules:
  0.0 75.8 jit_solution(14957198543462364027)
XLA Ops:
  0.0 6.0 %all-to-all-start = ((bf16[8,32,512]{2,1,0:T(8,128)(2,1)}), bf16[8,32,512]{2,1,0:T(8,128)(2,1)S(1)}, u32[]{:S(2)}, u32[]{:S(2)}) async-start(bf16[8,32,512]{2,1,0:T(8,128)(2,1)} %bitcast.19), calls=%async_computation | async-start | bytes 524288 | tf_op jit(solution)/shard_map/all_to_all | solution.py:296
  6.0 8.7 %all-to-all-done.x_ref = bf16[8,32,512]{2,1,0:T(8,128)(2,1)S(1)} async-done(((bf16[8,32,512]{2,1,0:T(8,128)(2,1)}), bf16[8,32,512]{2,1,0:T(8,128)(2,1)S(1)}, u32[]{:S(2)}, u32[]{:S(2)}) %all-to-all-start) | async-done | bytes 262176 | tf_op jit(solution)/shard_map/all_to_all | solution.py:296
  14.8 3.0 %shear_forward.1 = bf16[16,32,512]{2,1,0:T(8,128)(2,1)S(1)} custom-call(f32[4,8,8]{2,1,0:T(8,128)} %taps_hbm.3, s32[8,8]{1,0:T(8,128)} %offsets_hbm.3, bf16[8,32,512]{2,1,0:T(8,128)(2,1)S(1)} %all-to-all-done.x_ref, s32[1]{0:T(128)} %bitcast.refs_0_.strip_ref, s32[1]{0:T(128)} %bitcast.2.refs_1_), custom_call_target="tpu_custom_call" | custom-call | tf_op jit(solution)/shard_map/shear_forward/pallas_call | solution.py:96
  17.8 0.0 copy-start.1
  17.8 0.0 copy-start.2
  17.8 16.7 %all_to_all.20 = bf16[16,32,512]{2,1,0:T(8,128)(2,1)S(1)} all-to-all(bf16[16,32,512]{2,1,0:T(8,128)(2,1)S(1)} %shear_forward.1), channel_id=1, replica_groups={{1,33,65,97,129,161,193,225,2,34,66,98,130,162,194,226},{3,35,67,99,131..., dimensions={0} | all-to-all | bytes 1048576 | tf_op jit(solution)/shard_map/all_to_all | solution.py:299
  34.5 0.0 copy-start
  34.5 0.1 collective-permute-start
  35.3 0.8 %collective-permute-done.near_ref = bf16[2,128,512]{2,1,0:T(8,128)(2,1)S(1)} collective-permute-done((bf16[2,128,512]{2,1,0:T(8,128)(2,1)S(1)}, bf16[2,128,512]{2,1,0:T(8,128)(2,1)S(1)}, u32[]{:S(2)}, u32[]{:S(2)}) %collective-permute-start) | collective-permute-done | bytes 262176 | tf_op jit(solution)/shard_map/ppermute | solution.py:293
  36.1 0.0 copy-done.1
  36.1 0.0 copy-done.2
  36.1 0.0 copy-done
  36.1 6.5 %frames.1 = (f32[2,128,512]{2,1,0:T(8,128)S(1)}, bf16[2,128,512]{2,1,0:T(8,128)(2,1)S(1)}, bf16[2,2,128,512]{3,2,1,0:T(8,128)(2,1)S(1)}) custom-call(s32[1]{0:T(128)} %bitcast.refs_0_.strip_ref, s32[1,1]{1,0:T(1,128)S(6)} %copy.12.counts_ref, s32[1,4]{1,0:T(1,128)} %rows_hbm.1, s32[1,4]{1,0:T(1,128)} %columns_hbm.1, bf16[2,2,128,512]{3,2,1,0:T(8,128)(2,1)S(1)} %bitcast.15, ...), custom_call_target="tpu_custom_call" | custom-call | tf_op jit(solution)/shard_map/frames/pallas_call | solution.py:253
  42.6 0.1 collective-permute-start.1
  42.7 1.5 %collective-permute-done.1 = bf16[2,128,512]{2,1,0:T(8,128)(2,1)S(1)} collective-permute-done((bf16[2,128,512]{2,1,0:T(8,128)(2,1)S(1)}, bf16[2,128,512]{2,1,0:T(8,128)(2,1)S(1)}, u32[]{:S(2)}, u32[]{:S(2)}) %collective-permute-start.1) | collective-permute-done | bytes 262176 | tf_op jit(solution)/shard_map/ppermute | solution.py:293
  44.2 0.1 fusion.1
  44.3 15.5 %all_to_all.21.x_ref = bf16[16,32,512]{2,1,0:T(8,128)(2,1)S(1)} all-to-all(bf16[16,32,512]{2,1,0:T(8,128)(2,1)S(1)} %bitcast.16), channel_id=1, replica_groups={{1,33,65,97,129,161,193,225,2,34,66,98,130,162,194,226},{3,35,67,99,131..., dimensions={0} | all-to-all | bytes 1048576 | tf_op jit(solution)/shard_map/all_to_all | solution.py:299
  59.8 3.2 %shear_back.1 = bf16[8,32,512]{2,1,0:T(8,128)(2,1)S(1)} custom-call(f32[4,8,8]{2,1,0:T(8,128)} %taps_hbm.3, s32[8,8]{1,0:T(8,128)} %offsets_hbm.3, bf16[16,32,512]{2,1,0:T(8,128)(2,1)S(1)} %all_to_all.21.x_ref), custom_call_target="tpu_custom_call" | custom-call | tf_op jit(solution)/shard_map/shear_back/pallas_call | solution.py:96
  63.0 12.0 %all_to_all.22 = bf16[8,32,512]{2,1,0:T(8,128)(2,1)S(1)} all-to-all(bf16[8,32,512]{2,1,0:T(8,128)(2,1)S(1)} %shear_back.1), channel_id=1, replica_groups=mesh['ang'=8,'strip'=32] {'ang'}, dimensions={0} | all-to-all | bytes 524288 | tf_op jit(solution)/shard_map/all_to_all | solution.py:296
  75.0 0.9 %convert.1 = f32[1,2,128,512]{3,2,1,0:T(8,128)} convert(bf16[1,2,128,512]{3,2,1,0:T(8,128)(2,1)S(1)} %bitcast.18) | non-fusion elementwise | flops 131072 | bytes 786432 | tf_op jit(solution)/shard_map/convert_element_type | solution.py:309
  (1 shorter events, 0.0 us)
Async XLA Ops:
  0.0 14.8 %all-to-all-start = ((bf16[8,32,512]{2,1,0:T(8,128)(2,1)}), bf16[8,32,512]{2,1,0:T(8,128)(2,1)S(1)}, u32[]{:S(2)}, u32[]{:S(2)}) async-start(bf16[8,32,512]{2,1,0:T(8,128)(2,1)} %bitcast.19), calls=%async_computation | async-start | bytes 524288 | tf_op jit(solution)/shard_map/all_to_all | solution.py:296
  17.8 18.3 %copy-start.1 = (bf16[512,512]{1,0:T(8,128)(2,1)S(1)}, bf16[512,512]{1,0:T(8,128)(2,1)}, u32[]{:S(2)}) copy-start(bf16[512,512]{1,0:T(8,128)(2,1)} %constant.15.clone.inv_ref) | copy-start | bytes 1572868
  17.8 18.3 %copy-start.2 = (bf16[512,512]{1,0:T(8,128)(2,1)S(1)}, bf16[512,512]{1,0:T(8,128)(2,1)}, u32[]{:S(2)}) copy-start(bf16[512,512]{1,0:T(8,128)(2,1)} %constant.14.clone.fwd_ref) | copy-start | bytes 1572868
  34.5 1.7 %copy-start = (bf16[1,4,256,256]{3,2,1,0:T(8,128)(2,1)S(1)}, bf16[1,4,256,256]{3,2,1,0:T(8,128)(2,1)}, u32[]{:S(2)}) copy-start(bf16[1,4,256,256]{3,2,1,0:T(8,128)(2,1)} %param.17) | copy-start | bytes 1572868
  34.5 1.6 %collective-permute-start = (bf16[2,128,512]{2,1,0:T(8,128)(2,1)S(1)}, bf16[2,128,512]{2,1,0:T(8,128)(2,1)S(1)}, u32[]{:S(2)}, u32[]{:S(2)}) collective-permute-start(bf16[2,128,512]{2,1,0:T(8,128)(2,1)S(1)} %dynamic-slice_bitcast_fusion), channel_id=1, source_target_pairs={{0,1},{1,0},{2,3},{3,2},{4,5},{5,4},{6,7},{7,6},{8,9},{9,8},{10,11... | collective-permute-start | bytes 786440 | tf_op jit(solution)/shard_map/ppermute | solution.py:293
  42.6 1.6 %collective-permute-start.1 = (bf16[2,128,512]{2,1,0:T(8,128)(2,1)S(1)}, bf16[2,128,512]{2,1,0:T(8,128)(2,1)S(1)}, u32[]{:S(2)}, u32[]{:S(2)}) collective-permute-start(bf16[2,128,512]{2,1,0:T(8,128)(2,1)S(1)} %get-tuple-element.10), channel_id=1, source_target_pairs={{0,1},{1,0},{2,3},{3,2},{4,5},{5,4},{6,7},{7,6},{8,9},{9,8},{10,11... | collective-permute-start | bytes 786440 | tf_op jit(solution)/shard_map/ppermute | solution.py:293

commit v3 on v2

--- a/solution.py
+++ b/solution.py
@@ -53,6 +53,7 @@
         value = x_ref[s].astype(jnp.float32)
         for again in range(1, x_ref.shape[0] // count):
             value = value + x_ref[s + again * count].astype(jnp.float32)
+        value = value.astype(jnp.bfloat16).astype(jnp.float32)
         value = jnp.concatenate([value, jnp.zeros((rows, LANES), jnp.float32)], axis=1)
         for k in range(ntaps):
             moved = pltpu.roll(value, left - k, axis=1)
@@ -60,7 +61,7 @@
                 copies[s, k, j] = moved[:, j * LANES : (j + 1) * LANES]
         return 0
 
-    lax.fori_loop(0, count, lay_out, 0)
+    lax.fori_loop(0, count, lay_out, 0, unroll=4)
     get_taps.wait()
     get_offsets.wait()
     lane = lane_index((rows, LANES))
@@ -86,7 +87,7 @@
                 o_ref[d + again * count, :, pl.ds(j * LANES, LANES)] = out
         return 0
 
-    lax.fori_loop(0, count, one, 0)
+    lax.fori_loop(0, count, one, 0, unroll=4)
 
 
 def shear(x, taps, offsets, sign, copies, *ahead):

time: 76.8 us -> 76 us (0.990)
  Pallas kernels: 12.7 us -> 11.8 us
    pallas_call x2, Pallas kernels: 6.25 us -> 5.3 us  [shear(): pl.pallas_call(functools.partial(shear_body, sign, len(ahead)), out_shape...]
where the time goes in v3:
time: 76 us; the launch traced here: 74.7 us
  blocking collectives  43.9 us (58%)
  Pallas kernels  11.8 us (16%)
  waiting for transfers between devices  11.1 us (15%)
  starting transfers between devices  6.22 us (8%)
  other arithmetic  0.92 us (1%)
  between operations  0.76 us (1%)
    all_to_all x2, blocking collectives, pair_exchange(): lax.all_to_all(x, ('ang', 'strip'), 0, 0, axis_index_groups=groups, tiled...  32.3 us
    all_to_all x1, blocking collectives, exchange(): return lax.all_to_all(x, 'ang', 0, 0, tiled=True)  11.6 us
    all_to_all x1, waiting for transfers between devices, exchange(): return lax.all_to_all(x, 'ang', 0, 0, tiled=True)  8.73 us
    pallas_call x1, Pallas kernels, frames(): pl.pallas_call(functools.partial(frames_body, strips), out_shape=(jax.Sha...  6.52 us
    all_to_all x1, starting transfers between devices, exchange(): return lax.all_to_all(x, 'ang', 0, 0, tiled=True)  6.03 us
    pallas_call x2, Pallas kernels, shear(): pl.pallas_call(functools.partial(shear_body, sign, len(ahead)), out_shape...  5.3 us
    ppermute x2, waiting for transfers between devices, swap(): return lax.ppermute(x, 'strip', [(s, s ^ 1) for s in range(strips)])  2.36 us
  transfers between devices with their start and end apart: 3, of which 3 were waited for; matrix products, arithmetic and copies ran while one was open for 0% of the time, Pallas kernels for 0%

profile of v3, /device:TPU:2, one launch (start us, length us, event | category | flops | bytes accessed | tf_op | source)
XLA Modules:
  0.0 74.7 jit_solution(153407702070183897)
XLA Ops:
  0.0 6.0 %all-to-all-start = ((bf16[8,32,512]{2,1,0:T(8,128)(2,1)}), bf16[8,32,512]{2,1,0:T(8,128)(2,1)S(1)}, u32[]{:S(2)}, u32[]{:S(2)}) async-start(bf16[8,32,512]{2,1,0:T(8,128)(2,1)} %bitcast.19), calls=%async_computation | async-start | bytes 524288 | tf_op jit(solution)/shard_map/all_to_all | solution.py:297
  6.0 8.7 %all-to-all-done.x_ref = bf16[8,32,512]{2,1,0:T(8,128)(2,1)S(1)} async-done(((bf16[8,32,512]{2,1,0:T(8,128)(2,1)}), bf16[8,32,512]{2,1,0:T(8,128)(2,1)S(1)}, u32[]{:S(2)}, u32[]{:S(2)}) %all-to-all-start) | async-done | bytes 262176 | tf_op jit(solution)/shard_map/all_to_all | solution.py:297
  14.8 2.7 %shear_forward.1 = bf16[16,32,512]{2,1,0:T(8,128)(2,1)S(1)} custom-call(f32[4,8,8]{2,1,0:T(8,128)} %taps_hbm.3, s32[8,8]{1,0:T(8,128)} %offsets_hbm.3, bf16[8,32,512]{2,1,0:T(8,128)(2,1)S(1)} %all-to-all-done.x_ref, s32[1]{0:T(128)} %bitcast.refs_0_.strip_ref, s32[1]{0:T(128)} %bitcast.2.refs_1_), custom_call_target="tpu_custom_call" | custom-call | tf_op jit(solution)/shard_map/shear_forward/pallas_call | solution.py:97
  17.4 0.0 copy-start.1
  17.4 0.0 copy-start.2
  17.4 16.7 %all_to_all.20 = bf16[16,32,512]{2,1,0:T(8,128)(2,1)S(1)} all-to-all(bf16[16,32,512]{2,1,0:T(8,128)(2,1)S(1)} %shear_forward.1), channel_id=1, replica_groups={{1,33,65,97,129,161,193,225,2,34,66,98,130,162,194,226},{3,35,67,99,131..., dimensions={0} | all-to-all | bytes 1048576 | tf_op jit(solution)/shard_map/all_to_all | solution.py:300
  34.1 0.0 copy-start
  34.1 0.1 collective-permute-start
  34.9 0.8 %collective-permute-done.near_ref = bf16[2,128,512]{2,1,0:T(8,128)(2,1)S(1)} collective-permute-done((bf16[2,128,512]{2,1,0:T(8,128)(2,1)S(1)}, bf16[2,128,512]{2,1,0:T(8,128)(2,1)S(1)}, u32[]{:S(2)}, u32[]{:S(2)}) %collective-permute-start) | collective-permute-done | bytes 262176 | tf_op jit(solution)/shard_map/ppermute | solution.py:294
  35.7 0.0 copy-done.1
  35.8 0.0 copy-done.2
  35.8 0.0 copy-done
  35.8 6.5 %frames.1 = (f32[2,128,512]{2,1,0:T(8,128)S(1)}, bf16[2,128,512]{2,1,0:T(8,128)(2,1)S(1)}, bf16[2,2,128,512]{3,2,1,0:T(8,128)(2,1)S(1)}) custom-call(s32[1]{0:T(128)} %bitcast.refs_0_.strip_ref, s32[1,1]{1,0:T(1,128)S(6)} %copy.12.counts_ref, s32[1,4]{1,0:T(1,128)} %rows_hbm.1, s32[1,4]{1,0:T(1,128)} %columns_hbm.1, bf16[2,2,128,512]{3,2,1,0:T(8,128)(2,1)S(1)} %bitcast.15, ...), custom_call_target="tpu_custom_call" | custom-call | tf_op jit(solution)/shard_map/frames/pallas_call | solution.py:254
  42.3 0.1 collective-permute-start.1
  42.4 1.5 %collective-permute-done.1 = bf16[2,128,512]{2,1,0:T(8,128)(2,1)S(1)} collective-permute-done((bf16[2,128,512]{2,1,0:T(8,128)(2,1)S(1)}, bf16[2,128,512]{2,1,0:T(8,128)(2,1)S(1)}, u32[]{:S(2)}, u32[]{:S(2)}) %collective-permute-start.1) | collective-permute-done | bytes 262176 | tf_op jit(solution)/shard_map/ppermute | solution.py:294
  43.9 0.1 fusion.1
  44.0 15.6 %all_to_all.21.x_ref = bf16[16,32,512]{2,1,0:T(8,128)(2,1)S(1)} all-to-all(bf16[16,32,512]{2,1,0:T(8,128)(2,1)S(1)} %bitcast.16), channel_id=1, replica_groups={{1,33,65,97,129,161,193,225,2,34,66,98,130,162,194,226},{3,35,67,99,131..., dimensions={0} | all-to-all | bytes 1048576 | tf_op jit(solution)/shard_map/all_to_all | solution.py:300
  59.6 2.6 %shear_back.1 = bf16[8,32,512]{2,1,0:T(8,128)(2,1)S(1)} custom-call(f32[4,8,8]{2,1,0:T(8,128)} %taps_hbm.3, s32[8,8]{1,0:T(8,128)} %offsets_hbm.3, bf16[16,32,512]{2,1,0:T(8,128)(2,1)S(1)} %all_to_all.21.x_ref), custom_call_target="tpu_custom_call" | custom-call | tf_op jit(solution)/shard_map/shear_back/pallas_call | solution.py:97
  62.3 11.6 %all_to_all.22 = bf16[8,32,512]{2,1,0:T(8,128)(2,1)S(1)} all-to-all(bf16[8,32,512]{2,1,0:T(8,128)(2,1)S(1)} %shear_back.1), channel_id=1, replica_groups=mesh['ang'=8,'strip'=32] {'ang'}, dimensions={0} | all-to-all | bytes 524288 | tf_op jit(solution)/shard_map/all_to_all | solution.py:297
  73.9 0.9 %convert.1 = f32[1,2,128,512]{3,2,1,0:T(8,128)} convert(bf16[1,2,128,512]{3,2,1,0:T(8,128)(2,1)S(1)} %bitcast.18) | non-fusion elementwise | flops 131072 | bytes 786432 | tf_op jit(solution)/shard_map/convert_element_type | solution.py:310
  (1 shorter events, 0.0 us)
Async XLA Ops:
  0.0 14.8 %all-to-all-start = ((bf16[8,32,512]{2,1,0:T(8,128)(2,1)}), bf16[8,32,512]{2,1,0:T(8,128)(2,1)S(1)}, u32[]{:S(2)}, u32[]{:S(2)}) async-start(bf16[8,32,512]{2,1,0:T(8,128)(2,1)} %bitcast.19), calls=%async_computation | async-start | bytes 524288 | tf_op jit(solution)/shard_map/all_to_all | solution.py:297
  17.4 18.3 %copy-start.1 = (bf16[512,512]{1,0:T(8,128)(2,1)S(1)}, bf16[512,512]{1,0:T(8,128)(2,1)}, u32[]{:S(2)}) copy-start(bf16[512,512]{1,0:T(8,128)(2,1)} %constant.15.clone.inv_ref) | copy-start | bytes 1572868
  17.4 18.3 %copy-start.2 = (bf16[512,512]{1,0:T(8,128)(2,1)S(1)}, bf16[512,512]{1,0:T(8,128)(2,1)}, u32[]{:S(2)}) copy-start(bf16[512,512]{1,0:T(8,128)(2,1)} %constant.14.clone.fwd_ref) | copy-start | bytes 1572868
  34.1 1.7 %copy-start = (bf16[1,4,256,256]{3,2,1,0:T(8,128)(2,1)S(1)}, bf16[1,4,256,256]{3,2,1,0:T(8,128)(2,1)}, u32[]{:S(2)}) copy-start(bf16[1,4,256,256]{3,2,1,0:T(8,128)(2,1)} %param.17) | copy-start | bytes 1572868
  34.1 1.6 %collective-permute-start = (bf16[2,128,512]{2,1,0:T(8,128)(2,1)S(1)}, bf16[2,128,512]{2,1,0:T(8,128)(2,1)S(1)}, u32[]{:S(2)}, u32[]{:S(2)}) collective-permute-start(bf16[2,128,512]{2,1,0:T(8,128)(2,1)S(1)} %dynamic-slice_bitcast_fusion), channel_id=1, source_target_pairs={{0,1},{1,0},{2,3},{3,2},{4,5},{5,4},{6,7},{7,6},{8,9},{9,8},{10,11... | collective-permute-start | bytes 786440 | tf_op jit(solution)/shard_map/ppermute | solution.py:294
  42.3 1.6 %collective-permute-start.1 = (bf16[2,128,512]{2,1,0:T(8,128)(2,1)S(1)}, bf16[2,128,512]{2,1,0:T(8,128)(2,1)S(1)}, u32[]{:S(2)}, u32[]{:S(2)}) collective-permute-start(bf16[2,128,512]{2,1,0:T(8,128)(2,1)S(1)} %get-tuple-element.10), channel_id=1, source_target_pairs={{0,1},{1,0},{2,3},{3,2},{4,5},{5,4},{6,7},{7,6},{8,9},{9,8},{10,11... | collective-permute-start | bytes 786440 | tf_op jit(solution)/shard_map/ppermute | solution.py:294

commit v4 on v3

--- a/solution.py
+++ b/solution.py
@@ -165,7 +165,7 @@
         for at in spots:
             window = []
             for p in range(2):
-                turned = [pltpu.roll(ext[p, first + j, pl.ds(row + at, part), :], back, axis=1) for j in range(3)]
+                turned = [pltpu.roll(ext[p, first + j, pl.ds(row + at, part), :].astype(jnp.bfloat16), back, axis=1).astype(jnp.float32) for j in range(3)]
                 window.append([jnp.where(low, turned[j], turned[j + 1]) for j in range(2)])
             for j in range(2):
                 tile = pl.ds(j * LANES, LANES)

time: 76 us -> 75.6 us (level)
  blocking collectives: 43.9 us -> 47.9 us
  Pallas kernels: 11.8 us -> 7.96 us
    pallas_call x1, Pallas kernels: 6.52 us -> 2.66 us  [frames(): pl.pallas_call(functools.partial(frames_body, strips), out_shape=(jax.Sha...]
    all_to_all x2, blocking collectives: 32.3 us -> 35.7 us  [pair_exchange(): lax.all_to_all(x, ('ang', 'strip'), 0, 0, axis_index_groups=groups, tiled...]
where the time goes in v4:
time: 75.6 us; the launch traced here: 74.8 us
  blocking collectives  47.9 us (63%)
  waiting for transfers between devices  11 us (15%)
  Pallas kernels  7.96 us (11%)
  starting transfers between devices  6.31 us (8%)
  other arithmetic  0.92 us (1%)
    all_to_all x2, blocking collectives, pair_exchange(): lax.all_to_all(x, ('ang', 'strip'), 0, 0, axis_index_groups=groups, tiled...  35.7 us
    all_to_all x1, blocking collectives, exchange(): return lax.all_to_all(x, 'ang', 0, 0, tiled=True)  12.1 us
    all_to_all x1, waiting for transfers between devices, exchange(): return lax.all_to_all(x, 'ang', 0, 0, tiled=True)  8.73 us
    all_to_all x1, starting transfers between devices, exchange(): return lax.all_to_all(x, 'ang', 0, 0, tiled=True)  6.03 us
    pallas_call x2, Pallas kernels, shear(): pl.pallas_call(functools.partial(shear_body, sign, len(ahead)), out_shape...  5.3 us
    pallas_call x1, Pallas kernels, frames(): pl.pallas_call(functools.partial(frames_body, strips), out_shape=(jax.Sha...  2.66 us
    ppermute x2, waiting for transfers between devices, swap(): return lax.ppermute(x, 'strip', [(s, s ^ 1) for s in range(strips)])  2.27 us
  transfers between devices with their start and end apart: 3, of which 3 were waited for; matrix products, arithmetic and copies ran while one was open for 0% of the time, Pallas kernels for 0%

profile of v4, /device:TPU:2, one launch (start us, length us, event | category | flops | bytes accessed | tf_op | source)
XLA Modules:
  0.0 74.8 jit_solution(13648960845726061035)
XLA Ops:
  0.0 6.0 %all-to-all-start = ((bf16[8,32,512]{2,1,0:T(8,128)(2,1)}), bf16[8,32,512]{2,1,0:T(8,128)(2,1)S(1)}, u32[]{:S(2)}, u32[]{:S(2)}) async-start(bf16[8,32,512]{2,1,0:T(8,128)(2,1)} %bitcast.19), calls=%async_computation | async-start | bytes 524288 | tf_op jit(solution)/shard_map/all_to_all | solution.py:297
  6.0 8.7 %all-to-all-done.x_ref = bf16[8,32,512]{2,1,0:T(8,128)(2,1)S(1)} async-done(((bf16[8,32,512]{2,1,0:T(8,128)(2,1)}), bf16[8,32,512]{2,1,0:T(8,128)(2,1)S(1)}, u32[]{:S(2)}, u32[]{:S(2)}) %all-to-all-start) | async-done | bytes 262176 | tf_op jit(solution)/shard_map/all_to_all | solution.py:297
  14.8 2.7 %shear_forward.1 = bf16[16,32,512]{2,1,0:T(8,128)(2,1)S(1)} custom-call(f32[4,8,8]{2,1,0:T(8,128)} %taps_hbm.3, s32[8,8]{1,0:T(8,128)} %offsets_hbm.3, bf16[8,32,512]{2,1,0:T(8,128)(2,1)S(1)} %all-to-all-done.x_ref, s32[1]{0:T(128)} %bitcast.refs_0_.strip_ref, s32[1]{0:T(128)} %bitcast.2.refs_1_), custom_call_target="tpu_custom_call" | custom-call | tf_op jit(solution)/shard_map/shear_forward/pallas_call | solution.py:97
  17.4 0.0 copy-start.1
  17.4 0.0 copy-start.2
  17.4 16.7 %all_to_all.20 = bf16[16,32,512]{2,1,0:T(8,128)(2,1)S(1)} all-to-all(bf16[16,32,512]{2,1,0:T(8,128)(2,1)S(1)} %shear_forward.1), channel_id=1, replica_groups={{1,33,65,97,129,161,193,225,2,34,66,98,130,162,194,226},{3,35,67,99,131..., dimensions={0} | all-to-all | bytes 1048576 | tf_op jit(solution)/shard_map/all_to_all | solution.py:300
  34.1 0.0 copy-start
  34.1 0.1 collective-permute-start
  34.9 0.8 %collective-permute-done.near_ref = bf16[2,128,512]{2,1,0:T(8,128)(2,1)S(1)} collective-permute-done((bf16[2,128,512]{2,1,0:T(8,128)(2,1)S(1)}, bf16[2,128,512]{2,1,0:T(8,128)(2,1)S(1)}, u32[]{:S(2)}, u32[]{:S(2)}) %collective-permute-start) | collective-permute-done | bytes 262176 | tf_op jit(solution)/shard_map/ppermute | solution.py:294
  35.7 0.0 copy-done.1
  35.8 0.0 copy-done.2
  35.8 0.0 copy-done
  35.8 2.7 %frames.1 = (f32[2,128,512]{2,1,0:T(8,128)S(1)}, bf16[2,128,512]{2,1,0:T(8,128)(2,1)S(1)}, bf16[2,2,128,512]{3,2,1,0:T(8,128)(2,1)S(1)}) custom-call(s32[1]{0:T(128)} %bitcast.refs_0_.strip_ref, s32[1,1]{1,0:T(1,128)S(6)} %copy.12.counts_ref, s32[1,4]{1,0:T(1,128)} %rows_hbm.1, s32[1,4]{1,0:T(1,128)} %columns_hbm.1, bf16[2,2,128,512]{3,2,1,0:T(8,128)(2,1)S(1)} %bitcast.15, ...), custom_call_target="tpu_custom_call" | custom-call | tf_op jit(solution)/shard_map/frames/pallas_call | solution.py:254
  38.4 0.2 collective-permute-start.1
  38.6 1.4 %collective-permute-done.1 = bf16[2,128,512]{2,1,0:T(8,128)(2,1)S(1)} collective-permute-done((bf16[2,128,512]{2,1,0:T(8,128)(2,1)S(1)}, bf16[2,128,512]{2,1,0:T(8,128)(2,1)S(1)}, u32[]{:S(2)}, u32[]{:S(2)}) %collective-permute-start.1) | collective-permute-done | bytes 262176 | tf_op jit(solution)/shard_map/ppermute | solution.py:294
  40.1 0.1 fusion.1
  40.1 19.1 %all_to_all.21.x_ref = bf16[16,32,512]{2,1,0:T(8,128)(2,1)S(1)} all-to-all(bf16[16,32,512]{2,1,0:T(8,128)(2,1)S(1)} %bitcast.16), channel_id=1, replica_groups={{1,33,65,97,129,161,193,225,2,34,66,98,130,162,194,226},{3,35,67,99,131..., dimensions={0} | all-to-all | bytes 1048576 | tf_op jit(solution)/shard_map/all_to_all | solution.py:300
  59.2 2.6 %shear_back.1 = bf16[8,32,512]{2,1,0:T(8,128)(2,1)S(1)} custom-call(f32[4,8,8]{2,1,0:T(8,128)} %taps_hbm.3, s32[8,8]{1,0:T(8,128)} %offsets_hbm.3, bf16[16,32,512]{2,1,0:T(8,128)(2,1)S(1)} %all_to_all.21.x_ref), custom_call_target="tpu_custom_call" | custom-call | tf_op jit(solution)/shard_map/shear_back/pallas_call | solution.py:97
  61.9 12.1 %all_to_all.22 = bf16[8,32,512]{2,1,0:T(8,128)(2,1)S(1)} all-to-all(bf16[8,32,512]{2,1,0:T(8,128)(2,1)S(1)} %shear_back.1), channel_id=1, replica_groups=mesh['ang'=8,'strip'=32] {'ang'}, dimensions={0} | all-to-all | bytes 524288 | tf_op jit(solution)/shard_map/all_to_all | solution.py:297
  74.0 0.9 %convert.1 = f32[1,2,128,512]{3,2,1,0:T(8,128)} convert(bf16[1,2,128,512]{3,2,1,0:T(8,128)(2,1)S(1)} %bitcast.18) | non-fusion elementwise | flops 131072 | bytes 786432 | tf_op jit(solution)/shard_map/convert_element_type | solution.py:310
  (1 shorter events, 0.0 us)
Async XLA Ops:
  0.0 14.8 %all-to-all-start = ((bf16[8,32,512]{2,1,0:T(8,128)(2,1)}), bf16[8,32,512]{2,1,0:T(8,128)(2,1)S(1)}, u32[]{:S(2)}, u32[]{:S(2)}) async-start(bf16[8,32,512]{2,1,0:T(8,128)(2,1)} %bitcast.19), calls=%async_computation | async-start | bytes 524288 | tf_op jit(solution)/shard_map/all_to_all | solution.py:297
  17.4 18.3 %copy-start.1 = (bf16[512,512]{1,0:T(8,128)(2,1)S(1)}, bf16[512,512]{1,0:T(8,128)(2,1)}, u32[]{:S(2)}) copy-start(bf16[512,512]{1,0:T(8,128)(2,1)} %constant.15.clone.inv_ref) | copy-start | bytes 1572868
  17.4 18.3 %copy-start.2 = (bf16[512,512]{1,0:T(8,128)(2,1)S(1)}, bf16[512,512]{1,0:T(8,128)(2,1)}, u32[]{:S(2)}) copy-start(bf16[512,512]{1,0:T(8,128)(2,1)} %constant.14.clone.fwd_ref) | copy-start | bytes 1572868
  34.1 1.7 %copy-start = (bf16[1,4,256,256]{3,2,1,0:T(8,128)(2,1)S(1)}, bf16[1,4,256,256]{3,2,1,0:T(8,128)(2,1)}, u32[]{:S(2)}) copy-start(bf16[1,4,256,256]{3,2,1,0:T(8,128)(2,1)} %param.17) | copy-start | bytes 1572868
  34.1 1.6 %collective-permute-start = (bf16[2,128,512]{2,1,0:T(8,128)(2,1)S(1)}, bf16[2,128,512]{2,1,0:T(8,128)(2,1)S(1)}, u32[]{:S(2)}, u32[]{:S(2)}) collective-permute-start(bf16[2,128,512]{2,1,0:T(8,128)(2,1)S(1)} %dynamic-slice_bitcast_fusion), channel_id=1, source_target_pairs={{0,1},{1,0},{2,3},{3,2},{4,5},{5,4},{6,7},{7,6},{8,9},{9,8},{10,11... | collective-permute-start | bytes 786440 | tf_op jit(solution)/shard_map/ppermute | solution.py:294
  38.4 1.6 %collective-permute-start.1 = (bf16[2,128,512]{2,1,0:T(8,128)(2,1)S(1)}, bf16[2,128,512]{2,1,0:T(8,128)(2,1)S(1)}, u32[]{:S(2)}, u32[]{:S(2)}) collective-permute-start(bf16[2,128,512]{2,1,0:T(8,128)(2,1)S(1)} %get-tuple-element.10), channel_id=1, source_target_pairs={{0,1},{1,0},{2,3},{3,2},{4,5},{5,4},{6,7},{7,6},{8,9},{9,8},{10,11... | collective-permute-start | bytes 786440 | tf_op jit(solution)/shard_map/ppermute | solution.py:294

commit v5 on v4

--- a/solution.py
+++ b/solution.py
@@ -102,7 +102,7 @@
             pl.BlockSpec(memory_space=pltpu.HBM),
             pl.BlockSpec(memory_space=VMEM),
         ]
-        + [pl.BlockSpec(memory_space=SMEM)] * len(ahead),
+        + [pl.BlockSpec(memory_space=SMEM if x.dtype == jnp.int32 else VMEM) for x in ahead],
         out_specs=pl.BlockSpec(memory_space=VMEM),
         scratch_shapes=[
             SMEM(taps.shape, taps.dtype),
@@ -116,21 +116,13 @@
 
 
 def frames_body(
-    strips, strip_ref, counts_ref, rows_hbm, columns_hbm, pair_ref, near_ref, probe_hbm, fwd_ref, inv_ref, amp_ref,
+    strips, strip_ref, counts_ref, rows_ref, columns_ref, pair_ref, near_ref, probe_ref, fwd_ref, inv_ref, amp_ref,
     mid_ref, to_near_ref, send_ref,
-    ready, rows_ref, columns_ref, probe_ref, ext, placed,
+    ext, placed,
     column_a, column_b, side_a, side_b, wave_a,
 ):
     length = probe_ref.shape[1]
     strip, width = near_ref.shape[1:]
-    pairs = [
-        (rows_hbm, rows_ref),
-        (columns_hbm, columns_ref),
-        (probe_hbm, probe_ref),
-    ]
-    gets = [pltpu.make_async_copy(src, dst, ready.at[i]) for i, (src, dst) in enumerate(pairs)]
-    for get in gets:
-        get.start()
     me = strip_ref[0]
     odd = me & 1
     has_far = (me > 0) & (me < strips - 1)
@@ -146,8 +138,6 @@
             ext[p, j, pl.ds(far_row, strip), :] = jnp.where(has_far, far, 0.0)
     placed[...] = jnp.zeros_like(placed)
     wave_a[...] = jnp.zeros_like(wave_a)
-    for get in gets:
-        get.wait()
     part = 16
     lane = lane_index((part, LANES))
     count = counts_ref[0, 0]
@@ -249,7 +239,6 @@
     parts, strip, width = near.shape
     fwd, inv = (jnp.asarray(m) for m in dft_blocks(length))
     smem = pl.BlockSpec(memory_space=SMEM)
-    hbm = pl.BlockSpec(memory_space=pltpu.HBM)
     vmem = pl.BlockSpec(memory_space=VMEM)
     return pl.pallas_call(
         functools.partial(frames_body, strips),
@@ -258,13 +247,9 @@
             jax.ShapeDtypeStruct(near.shape, jnp.bfloat16),
             jax.ShapeDtypeStruct(pair.shape, jnp.bfloat16),
         ),
-        in_specs=[smem] * 2 + [hbm] * 2 + [vmem] * 2 + [hbm] + [vmem] * 3,
+        in_specs=[smem] * 4 + [vmem] * 6,
         out_specs=(vmem,) * 3,
         scratch_shapes=[
-            pltpu.SemaphoreType.DMA((3,)),
-            SMEM(rows.shape, rows.dtype),
-            SMEM(columns.shape, columns.dtype),
-            VMEM(probe.shape, probe.dtype),
             VMEM((parts, width // LANES + 1, 3 * strip, LANES), jnp.float32),
             VMEM((parts, width // LANES + 1, 3 * strip, LANES), jnp.float32),
             VMEM((2 * length, length), jnp.bfloat16),
@@ -275,7 +260,7 @@
         ],
         compiler_params=pltpu.CompilerParams(vmem_limit_bytes=32 << 20),
         name="frames",
-    )(me, counts, in_hbm(rows), in_hbm(columns), pair, near, in_hbm(probe), fwd, inv, amplitudes)
+    )(me, counts, rows, columns, pair, near, probe, fwd, inv, amplitudes)
 
 
 def per_device(slab, taps, offsets, probe, scan_rows, scan_columns, counts, amplitudes):
@@ -300,7 +285,7 @@
         return lax.all_to_all(x, ("ang", "strip"), 0, 0, axis_index_groups=groups, tiled=True)
 
     mixed = exchange(slab.reshape(angles, block, width))
-    pair = pair_exchange(shear(mixed, taps, offsets, 1, 2, place, half)).reshape(2, parts, rows, width)
+    pair = pair_exchange(shear(mixed, taps, offsets, 1, 2, place, half, probe)).reshape(2, parts, rows, width)
     near = swap(lax.dynamic_index_in_dim(pair, own_half, 0, keepdims=False))
     mid, to_near, send = frames(place, strips, counts, scan_rows, scan_columns, pair, near, probe, amplitudes[0])
     own = (mid + swap(to_near).astype(jnp.float32)).astype(jnp.bfloat16)

time: 75.6 us -> 75.7 us (level)
  Pallas kernels: 7.96 us -> 9.13 us
  blocking collectives: 47.9 us -> 47 us
    pallas_call x1, Pallas kernels: 2.66 us -> 3.83 us  [frames(): pl.pallas_call(functools.partial(frames_body, strips), out_shape=(jax.Sha...]
where the time goes in v5:
time: 75.7 us; the launch traced here: 75.3 us
  blocking collectives  47 us (62%)
  waiting for transfers between devices  10.8 us (14%)
  Pallas kernels  9.13 us (12%)
  starting transfers between devices  6.58 us (9%)
  other arithmetic  0.92 us (1%)
  between operations  0.78 us (1%)
    all_to_all x2, blocking collectives, pair_exchange(): lax.all_to_all(x, ('ang', 'strip'), 0, 0, axis_index_groups=groups, tiled...  35 us
    all_to_all x1, blocking collectives, exchange(): return lax.all_to_all(x, 'ang', 0, 0, tiled=True)  12 us
    all_to_all x1, waiting for transfers between devices, exchange(): return lax.all_to_all(x, 'ang', 0, 0, tiled=True)  8.73 us
    all_to_all x1, starting transfers between devices, exchange(): return lax.all_to_all(x, 'ang', 0, 0, tiled=True)  6.16 us
    pallas_call x2, Pallas kernels, shear(): pl.pallas_call(functools.partial(shear_body, sign, len(ahead)), out_shape...  5.3 us
    pallas_call x1, Pallas kernels, frames(): pl.pallas_call(functools.partial(frames_body, strips), out_shape=(jax.Sha...  3.83 us
    ppermute x2, waiting for transfers between devices, swap(): return lax.ppermute(x, 'strip', [(s, s ^ 1) for s in range(strips)])  2.11 us
  transfers between devices with their start and end apart: 3, of which 3 were waited for; matrix products, arithmetic and copies ran while one was open for 0% of the time, Pallas kernels for 0%

profile of v5, /device:TPU:2, one launch (start us, length us, event | category | flops | bytes accessed | tf_op | source)
XLA Modules:
  0.0 75.3 jit_solution(10092852808604345937)
XLA Ops:
  0.0 0.0 copy-start
  0.0 6.2 %all-to-all-start = ((bf16[8,32,512]{2,1,0:T(8,128)(2,1)}), bf16[8,32,512]{2,1,0:T(8,128)(2,1)S(1)}, u32[]{:S(2)}, u32[]{:S(2)}) async-start(bf16[8,32,512]{2,1,0:T(8,128)(2,1)} %bitcast.19), calls=%async_computation | async-start | bytes 524288 | tf_op jit(solution)/shard_map/all_to_all | solution.py:282
  6.2 8.7 %all-to-all-done.x_ref = bf16[8,32,512]{2,1,0:T(8,128)(2,1)S(1)} async-done(((bf16[8,32,512]{2,1,0:T(8,128)(2,1)}), bf16[8,32,512]{2,1,0:T(8,128)(2,1)S(1)}, u32[]{:S(2)}, u32[]{:S(2)}) %all-to-all-start) | async-done | bytes 262176 | tf_op jit(solution)/shard_map/all_to_all | solution.py:282
  14.9 0.0 copy-done
  14.9 2.7 %shear_forward.1 = bf16[16,32,512]{2,1,0:T(8,128)(2,1)S(1)} custom-call(f32[4,8,8]{2,1,0:T(8,128)} %taps_hbm.3, s32[8,8]{1,0:T(8,128)} %offsets_hbm.3, bf16[8,32,512]{2,1,0:T(8,128)(2,1)S(1)} %all-to-all-done.x_ref, s32[1]{0:T(128)} %bitcast.refs_0_.strip_ref, s32[1]{0:T(128)} %bitcast.2.refs_1_, bf16[2,256,256]{2,1,0:T(8,128)(2,1)S(1)} %copy-done), custom_call_target="tpu_custom_call" | custom-call | tf_op jit(solution)/shard_map/shear_forward/pallas_call | solution.py:97
  17.6 0.0 copy-start.2
  17.6 0.0 copy-start.3
  17.6 16.7 %all_to_all.20 = bf16[16,32,512]{2,1,0:T(8,128)(2,1)S(1)} all-to-all(bf16[16,32,512]{2,1,0:T(8,128)(2,1)S(1)} %shear_forward.1), channel_id=1, replica_groups={{1,33,65,97,129,161,193,225,2,34,66,98,130,162,194,226},{3,35,67,99,131..., dimensions={0} | all-to-all | bytes 1048576 | tf_op jit(solution)/shard_map/all_to_all | solution.py:285
  34.2 0.0 copy-start.1
  34.3 0.1 collective-permute-start
  35.0 0.0 copy-start.4
  35.1 0.0 copy-start.5
  35.1 0.8 %collective-permute-done.near_ref = bf16[2,128,512]{2,1,0:T(8,128)(2,1)S(1)} collective-permute-done((bf16[2,128,512]{2,1,0:T(8,128)(2,1)S(1)}, bf16[2,128,512]{2,1,0:T(8,128)(2,1)S(1)}, u32[]{:S(2)}, u32[]{:S(2)}) %collective-permute-start) | collective-permute-done | bytes 262176 | tf_op jit(solution)/shard_map/ppermute | solution.py:279
  35.9 0.0 copy-done.2
  35.9 0.0 copy-done.3
  35.9 0.0 copy-done.1
  35.9 0.0 copy-done.4
  35.9 0.0 copy-done.5
  35.9 3.8 %frames.1 = (f32[2,128,512]{2,1,0:T(8,128)S(1)}, bf16[2,128,512]{2,1,0:T(8,128)(2,1)S(1)}, bf16[2,2,128,512]{3,2,1,0:T(8,128)(2,1)S(1)}) custom-call(s32[1]{0:T(128)} %bitcast.refs_0_.strip_ref, s32[1,1]{1,0:T(1,128)S(6)} %copy.12.counts_ref, s32[1,4]{1,0:T(1,128)S(1)} %copy-done.4, s32[1,4]{1,0:T(1,128)S(1)} %copy-done.5, ...), custom_call_target="tpu_custom_call" | custom-call | tf_op jit(solution)/shard_map/frames/pallas_call | solution.py:243
  39.8 0.3 collective-permute-start.1
  40.1 1.3 %collective-permute-done.1 = bf16[2,128,512]{2,1,0:T(8,128)(2,1)S(1)} collective-permute-done((bf16[2,128,512]{2,1,0:T(8,128)(2,1)S(1)}, bf16[2,128,512]{2,1,0:T(8,128)(2,1)S(1)}, u32[]{:S(2)}, u32[]{:S(2)}) %collective-permute-start.1) | collective-permute-done | bytes 262176 | tf_op jit(solution)/shard_map/ppermute | solution.py:279
  41.4 0.1 fusion.1
  41.4 18.3 %all_to_all.21.x_ref = bf16[16,32,512]{2,1,0:T(8,128)(2,1)S(1)} all-to-all(bf16[16,32,512]{2,1,0:T(8,128)(2,1)S(1)} %bitcast.16), channel_id=1, replica_groups={{1,33,65,97,129,161,193,225,2,34,66,98,130,162,194,226},{3,35,67,99,131..., dimensions={0} | all-to-all | bytes 1048576 | tf_op jit(solution)/shard_map/all_to_all | solution.py:285
  59.8 2.6 %shear_back.1 = bf16[8,32,512]{2,1,0:T(8,128)(2,1)S(1)} custom-call(f32[4,8,8]{2,1,0:T(8,128)} %taps_hbm.3, s32[8,8]{1,0:T(8,128)} %offsets_hbm.3, bf16[16,32,512]{2,1,0:T(8,128)(2,1)S(1)} %all_to_all.21.x_ref), custom_call_target="tpu_custom_call" | custom-call | tf_op jit(solution)/shard_map/shear_back/pallas_call | solution.py:97
  62.4 12.0 %all_to_all.22 = bf16[8,32,512]{2,1,0:T(8,128)(2,1)S(1)} all-to-all(bf16[8,32,512]{2,1,0:T(8,128)(2,1)S(1)} %shear_back.1), channel_id=1, replica_groups=mesh['ang'=8,'strip'=32] {'ang'}, dimensions={0} | all-to-all | bytes 524288 | tf_op jit(solution)/shard_map/all_to_all | solution.py:282
  74.4 0.9 %convert.1 = f32[1,2,128,512]{3,2,1,0:T(8,128)} convert(bf16[1,2,128,512]{3,2,1,0:T(8,128)(2,1)S(1)} %bitcast.18) | non-fusion elementwise | flops 131072 | bytes 786432 | tf_op jit(solution)/shard_map/convert_element_type | solution.py:295
  (1 shorter events, 0.0 us)
Async XLA Ops:
  0.0 14.9 %copy-start = (bf16[2,256,256]{2,1,0:T(8,128)(2,1)S(1)}, bf16[2,256,256]{2,1,0:T(8,128)(2,1)}, u32[]{:S(2)}) copy-start(bf16[2,256,256]{2,1,0:T(8,128)(2,1)} %probe_ref.1) | copy-start | bytes 786436
  0.0 14.9 %all-to-all-start = ((bf16[8,32,512]{2,1,0:T(8,128)(2,1)}), bf16[8,32,512]{2,1,0:T(8,128)(2,1)S(1)}, u32[]{:S(2)}, u32[]{:S(2)}) async-start(bf16[8,32,512]{2,1,0:T(8,128)(2,1)} %bitcast.19), calls=%async_computation | async-start | bytes 524288 | tf_op jit(solution)/shard_map/all_to_all | solution.py:282
  17.6 18.3 %copy-start.2 = (bf16[512,512]{1,0:T(8,128)(2,1)S(1)}, bf16[512,512]{1,0:T(8,128)(2,1)}, u32[]{:S(2)}) copy-start(bf16[512,512]{1,0:T(8,128)(2,1)} %constant.15.clone.inv_ref) | copy-start | bytes 1572868
  17.6 18.3 %copy-start.3 = (bf16[512,512]{1,0:T(8,128)(2,1)S(1)}, bf16[512,512]{1,0:T(8,128)(2,1)}, u32[]{:S(2)}) copy-start(bf16[512,512]{1,0:T(8,128)(2,1)} %constant.14.clone.fwd_ref) | copy-start | bytes 1572868
  34.2 1.7 %copy-start.1 = (bf16[1,4,256,256]{3,2,1,0:T(8,128)(2,1)S(1)}, bf16[1,4,256,256]{3,2,1,0:T(8,128)(2,1)}, u32[]{:S(2)}) copy-start(bf16[1,4,256,256]{3,2,1,0:T(8,128)(2,1)} %param.17) | copy-start | bytes 1572868
  34.3 1.6 %collective-permute-start = (bf16[2,128,512]{2,1,0:T(8,128)(2,1)S(1)}, bf16[2,128,512]{2,1,0:T(8,128)(2,1)S(1)}, u32[]{:S(2)}, u32[]{:S(2)}) collective-permute-start(bf16[2,128,512]{2,1,0:T(8,128)(2,1)S(1)} %dynamic-slice_bitcast_fusion), channel_id=1, source_target_pairs={{0,1},{1,0},{2,3},{3,2},{4,5},{5,4},{6,7},{7,6},{8,9},{9,8},{10,11... | collective-permute-start | bytes 786440 | tf_op jit(solution)/shard_map/ppermute | solution.py:279
  35.0 0.8 %copy-start.4 = (s32[1,4]{1,0:T(1,128)S(1)}, s32[1,4]{1,0:T(1,128)}, u32[]{:S(2)}) copy-start(s32[1,4]{1,0:T(1,128)} %rows_ref.1) | copy-start | bytes 52
  35.1 0.8 %copy-start.5 = (s32[1,4]{1,0:T(1,128)S(1)}, s32[1,4]{1,0:T(1,128)}, u32[]{:S(2)}) copy-start(s32[1,4]{1,0:T(1,128)} %columns_ref.1) | copy-start | bytes 52
  39.8 1.6 %collective-permute-start.1 = (bf16[2,128,512]{2,1,0:T(8,128)(2,1)S(1)}, bf16[2,128,512]{2,1,0:T(8,128)(2,1)S(1)}, u32[]{:S(2)}, u32[]{:S(2)}) collective-permute-start(bf16[2,128,512]{2,1,0:T(8,128)(2,1)S(1)} %get-tuple-element.10), channel_id=1, source_target_pairs={{0,1},{1,0},{2,3},{3,2},{4,5},{5,4},{6,7},{7,6},{8,9},{9,8},{10,11... | collective-permute-start | bytes 786440 | tf_op jit(solution)/shard_map/ppermute | solution.py:279
